TPU v7x, 256 devices: a whole 4x4x8 slice. The times are simulated.
256 devices in a mesh: ctx: 64 (over z, x, core), ch: 4 (over y).
Axes of the slice: x: 4, y: 4, z: 8, core: 2. Of those that a mesh axis runs over, the one named last changes fastest.
Arguments:
- value_in: bfloat16 [256, 131072], P('ch', 'ctx'), may hold values from -6 to 6
- key_gate: bfloat16 [256, 131072], P('ch', 'ctx'), may hold values from -6 to 6
- query_gate: bfloat16 [256, 131072], P('ch', 'ctx'), may hold values from -6 to 6
- filter_taps: float32 [256, 131072], P('ch', 'ctx'), may hold values from -0.015625 to 0.015625
- skip_gain: float32 [256], P('ch'), may hold values from 0.5 to 1.5
- out_weight: bfloat16 [256, 256], P(None, 'ch'), may hold values from -0.375 to 0.375
Outputs:
- mixed_out: bfloat16 [256, 131072], P('ch', 'ctx')
All inputs are finite; a program needn't handle non-finite values.
Results may differ from a plain program's by a relative error of at most 0.0049.
Values may be sent and summed in bfloat16 or wider, within the bound.
A program may use at most 64 MiB of HBM per device.

v0:
```python
import math

import jax
import jax.numpy as jnp
from jax import lax
from jax.sharding import PartitionSpec as P

TWO_PI = 2.0 * math.pi
PRECISE = lax.Precision.HIGHEST


def partner(x, axis, bit):
    return lax.ppermute(x, axis, [(i, i ^ 1 << bit) for i in range(lax.axis_size(axis))])


def unit_table(row_count, column_count, length, sign_value):
    row_index = lax.broadcasted_iota(jnp.int32, (row_count, column_count), 0)
    column_index = lax.broadcasted_iota(jnp.int32, (row_count, column_count), 1)
    angles = (row_index * column_index % length).astype(jnp.float32) * (TWO_PI / length)
    return (jnp.cos(angles), sign_value * jnp.sin(angles))


def rotate(real_part, imaginary, angles):
    cosine_part = jnp.cos(angles)
    sine_part = jnp.sin(angles)
    return (
        real_part * cosine_part - imaginary * sine_part,
        imaginary * cosine_part + real_part * sine_part,
    )


def transform_last(real_part, imaginary, length, sign_value):
    cosine_table, sine_table = unit_table(length, length, length, sign_value)

    def multiply(operand, table):
        return jnp.einsum("...a,ak->...k", operand, table, precision=PRECISE)

    return (
        multiply(real_part, cosine_table) - multiply(imaginary, sine_table),
        multiply(imaginary, cosine_table) + multiply(real_part, sine_table),
    )


def transform_rows(real_part, imaginary, length, sign_value):
    cosine_table, sine_table = unit_table(length, length, length, sign_value)

    def multiply(operand, table):
        return jnp.einsum("...ab,ak->...kb", operand, table, precision=PRECISE)

    return (
        multiply(real_part, cosine_table) - multiply(imaginary, sine_table),
        multiply(imaginary, cosine_table) + multiply(real_part, sine_table),
    )


def twiddle_angles(outer_size, inner_size, sign_value):
    length = outer_size * inner_size
    row_index = lax.broadcasted_iota(jnp.int32, (outer_size, inner_size), 0)
    column_index = lax.broadcasted_iota(jnp.int32, (outer_size, inner_size), 1)
    return sign_value * (row_index * column_index % length).astype(jnp.float32) * (TWO_PI / length)


def local_forward(real_part, imaginary):
    length = real_part.shape[-1]
    inner_size = min(length, 128)
    outer_size = length // inner_size
    new_shape = real_part.shape[:-1] + (outer_size, inner_size)
    real_part = real_part.reshape(new_shape)
    imaginary = imaginary.reshape(new_shape)
    real_part, imaginary = transform_rows(real_part, imaginary, outer_size, -1.0)
    real_part, imaginary = rotate(
        real_part, imaginary, twiddle_angles(outer_size, inner_size, -1.0)
    )
    return transform_last(real_part, imaginary, inner_size, -1.0)


def local_inverse(real_part, imaginary):
    outer_size, inner_size = (real_part.shape[-2], real_part.shape[-1])
    real_part, imaginary = transform_last(real_part, imaginary, inner_size, 1.0)
    real_part, imaginary = rotate(real_part, imaginary, twiddle_angles(outer_size, inner_size, 1.0))
    real_part, imaginary = transform_rows(real_part, imaginary, outer_size, 1.0)
    new_shape = real_part.shape[:-2] + (outer_size * inner_size,)
    return (real_part.reshape(new_shape), imaginary.reshape(new_shape))


def spectral_product(real_part, imaginary, frequencies, padded_length):
    length = real_part.shape[-1]
    positions = lax.broadcasted_iota(jnp.int32, (frequencies.shape[0], length), 1)
    phases = (positions * frequencies[:, None] % padded_length).astype(jnp.float32) * (
        TWO_PI / padded_length
    )
    real_part, imaginary = rotate(real_part, imaginary, -phases[None, :, None, :])
    real_part, imaginary = local_forward(real_part, imaginary)
    product_real = real_part[0] * real_part[1] - imaginary[0] * imaginary[1]
    product_imaginary = real_part[0] * imaginary[1] + imaginary[0] * real_part[1]
    product_real, product_imaginary = local_inverse(product_real, product_imaginary)
    return rotate(product_real, product_imaginary, phases[:, None, :])


def bit_reverse(device_index, levels):
    result_index = jnp.zeros((), jnp.int32)
    for bit_index in range(levels):
        result_index = result_index | (device_index >> bit_index & 1) << levels - 1 - bit_index
    return result_index


def on_device(value_in, key_gate, query_gate, filter_taps, skip_gain, out_weight):
    devices = lax.axis_size("ctx")
    device_index = lax.axis_index("ctx")
    length = value_in.shape[1]
    padded_length = 2 * length * devices
    signal = value_in.astype(jnp.float32) * key_gate.astype(jnp.float32)
    stacked = jnp.stack([signal, filter_taps])
    levels = devices.bit_length() - 1
    half_phase = device_index.astype(jnp.float32) * (TWO_PI / (2 * devices))
    zeroes = jnp.zeros_like(stacked)
    real_part = jnp.stack([stacked, stacked * jnp.cos(half_phase)], axis=1)
    imaginary = jnp.stack([zeroes, -stacked * jnp.sin(half_phase)], axis=1)
    for bit_index in reversed(range(levels)):
        half_span = 1 << bit_index
        other_real, other_imaginary = partner((real_part, imaginary), "ctx", bit_index)
        is_lower = device_index >> bit_index & 1 == 1
        angles = -(device_index & half_span - 1).astype(jnp.float32) * (TWO_PI / (2 * half_span))
        delta_real, delta_imaginary = rotate(
            other_real - real_part, other_imaginary - imaginary, angles
        )
        real_part = jnp.where(is_lower, delta_real, real_part + other_real)
        imaginary = jnp.where(is_lower, delta_imaginary, imaginary + other_imaginary)
    frequencies = 2 * bit_reverse(device_index, levels) + jnp.arange(2, dtype=jnp.int32)
    product_real, product_imaginary = spectral_product(
        real_part, imaginary, frequencies, padded_length
    )
    for bit_index in range(levels):
        half_span = 1 << bit_index
        other_real, other_imaginary = partner((product_real, product_imaginary), "ctx", bit_index)
        is_lower = device_index >> bit_index & 1 == 1
        angles = (device_index & half_span - 1).astype(jnp.float32) * (TWO_PI / (2 * half_span))
        own_real, own_imaginary = rotate(product_real, product_imaginary, angles)
        turned_real, turned_imaginary = rotate(other_real, other_imaginary, angles)
        product_real = jnp.where(is_lower, other_real - own_real, product_real + turned_real)
        product_imaginary = jnp.where(
            is_lower, other_imaginary - own_imaginary, product_imaginary + turned_imaginary
        )
    phase_back = device_index.astype(jnp.float32) * (TWO_PI / (2 * devices))
    convolved = (
        product_real[0]
        + jnp.cos(phase_back) * product_real[1]
        - jnp.sin(phase_back) * product_imaginary[1]
    )
    convolved = convolved * (1.0 / padded_length)
    gated_values = (
        query_gate.astype(jnp.float32)
        * (convolved + skip_gain[:, None] * value_in.astype(jnp.float32))
    ).astype(jnp.bfloat16)
    mixed_out = lax.dot_general(
        out_weight,
        lax.all_gather(gated_values, "ch", axis=0, tiled=True),
        (((0,), (0,)), ((), ())),
        preferred_element_type=jnp.float32,
    )
    return mixed_out.astype(jnp.bfloat16)


def solution(mesh):
    placed = (
        P("ch", "ctx"),
        P("ch", "ctx"),
        P("ch", "ctx"),
        P("ch", "ctx"),
        P("ch"),
        P(None, "ch"),
    )
    return jax.shard_map(
        on_device, mesh=mesh, in_specs=placed, out_specs=P("ch", "ctx"), check_vma=False
    )
```

profile of v0, /device:TPU:1, one launch (start us, length us, event | category | flops | bytes accessed | tf_op | source)
XLA Modules:
  0.0 1118.7 jit_solution(3734244577662430579)
XLA Ops:
  10.8 7.7 collective-permute-start
  20.3 59.5 %collective-permute-done = f32[2,2,64,2048]{3,2,1,0:T(8,128)} collective-permute-done((f32[2,2,64,2048]{3,2,1,0:T(8,128)}, f32[2,2,64,2048]{3,2,1,0:T(8,128)}, u32[]{:S(2)}, u32[]{:S(2)}) %collective-permute-start) | collective-permute-done | bytes 2097184 | tf_op jit(solution)/shard_map/ppermute | solution.py:13
  79.8 91.8 %collective-permute-done.1 = f32[2,2,64,2048]{3,2,1,0:T(8,128)} collective-permute-done((f32[2,2,64,2048]{3,2,1,0:T(8,128)}, f32[2,2,64,2048]{3,2,1,0:T(8,128)}, u32[]{:S(2)}, u32[]{:S(2)}) %collective-permute-start.1) | collective-permute-done | bytes 2097184 | tf_op jit(solution)/shard_map/ppermute | solution.py:13
  171.6 5.2 add_select_fusion.10
  176.9 29.5 %collective-permute-start.2 = (f32[2,2,64,2048]{3,2,1,0:T(8,128)}, f32[2,2,64,2048]{3,2,1,0:T(8,128)S(1)}, u32[]{:S(2)}, u32[]{:S(2)}) collective-permute-start(f32[2,2,64,2048]{3,2,1,0:T(8,128)} %get-tuple-element.17), channel_id=1, source_target_pairs={{0,64},{4,68},{8,72},{12,76},{16,80},{20,84},{24,88},{28,92},{32,9... | collective-permute-start | bytes 6291464 | tf_op jit(solution)/shard_map/ppermute | solution.py:13
  206.5 134.0 %collective-permute-done.2 = f32[2,2,64,2048]{3,2,1,0:T(8,128)S(1)} collective-permute-done((f32[2,2,64,2048]{3,2,1,0:T(8,128)}, f32[2,2,64,2048]{3,2,1,0:T(8,128)S(1)}, u32[]{:S(2)}, u32[]{:S(2)}) %collective-permute-start.2) | collective-permute-done | bytes 2097184 | tf_op jit(solution)/shard_map/ppermute | solution.py:13
  341.8 43.7 %collective-permute-done.3 = f32[2,2,64,2048]{3,2,1,0:T(8,128)} collective-permute-done((f32[2,2,64,2048]{3,2,1,0:T(8,128)}, f32[2,2,64,2048]{3,2,1,0:T(8,128)}, u32[]{:S(2)}, u32[]{:S(2)}) %collective-permute-start.3) | collective-permute-done | bytes 2097184 | tf_op jit(solution)/shard_map/ppermute | solution.py:13
  385.5 6.0 add_select_fusion.8
  391.6 2.5 collective-permute-start.4
  394.2 44.6 %collective-permute-done.4 = f32[2,2,64,2048]{3,2,1,0:T(8,128)} collective-permute-done((f32[2,2,64,2048]{3,2,1,0:T(8,128)}, f32[2,2,64,2048]{3,2,1,0:T(8,128)}, u32[]{:S(2)}, u32[]{:S(2)}) %collective-permute-start.4) | collective-permute-done | bytes 2097184 | tf_op jit(solution)/shard_map/ppermute | solution.py:13
  438.9 44.8 %collective-permute-done.5 = f32[2,2,64,2048]{3,2,1,0:T(8,128)} collective-permute-done((f32[2,2,64,2048]{3,2,1,0:T(8,128)S(1)}, f32[2,2,64,2048]{3,2,1,0:T(8,128)}, u32[]{:S(2)}, u32[]{:S(2)}) %collective-permute-start.5) | collective-permute-done | bytes 2097184 | tf_op jit(solution)/shard_map/ppermute | solution.py:13
  483.7 6.1 add_select_fusion.6
  489.8 2.7 collective-permute-start.6
  492.9 43.6 %collective-permute-done.6 = f32[2,2,64,2048]{3,2,1,0:T(8,128)S(1)} collective-permute-done((f32[2,2,64,2048]{3,2,1,0:T(8,128)}, f32[2,2,64,2048]{3,2,1,0:T(8,128)S(1)}, u32[]{:S(2)}, u32[]{:S(2)}) %collective-permute-start.6) | collective-permute-done | bytes 2097184 | tf_op jit(solution)/shard_map/ppermute | solution.py:13
  537.8 43.7 %collective-permute-done.7 = f32[2,2,64,2048]{3,2,1,0:T(8,128)} collective-permute-done((f32[2,2,64,2048]{3,2,1,0:T(8,128)}, f32[2,2,64,2048]{3,2,1,0:T(8,128)}, u32[]{:S(2)}, u32[]{:S(2)}) %collective-permute-start.7) | collective-permute-done | bytes 2097184 | tf_op jit(solution)/shard_map/ppermute | solution.py:13
  581.5 6.0 add_select_fusion.4
  589.2 42.8 %collective-permute-done.8 = f32[2,2,64,2048]{3,2,1,0:T(8,128)} collective-permute-done((f32[2,2,64,2048]{3,2,1,0:T(8,128)}, f32[2,2,64,2048]{3,2,1,0:T(8,128)}, u32[]{:S(2)}, u32[]{:S(2)}) %collective-permute-start.8) | collective-permute-done | bytes 2097184 | tf_op jit(solution)/shard_map/ppermute | solution.py:13
  632.0 44.9 %collective-permute-done.9 = f32[2,2,64,2048]{3,2,1,0:T(8,128)} collective-permute-done((f32[2,2,64,2048]{3,2,1,0:T(8,128)S(1)}, f32[2,2,64,2048]{3,2,1,0:T(8,128)}, u32[]{:S(2)}, u32[]{:S(2)}) %collective-permute-start.9) | collective-permute-done | bytes 2097184 | tf_op jit(solution)/shard_map/ppermute | solution.py:13
  676.9 6.1 add_select_fusion.2
  683.0 4.2 collective-permute-start.10
  688.1 3.2 collective-permute-done.10
  691.3 3.1 collective-permute-done.11
  694.4 4.3 multiply_add_fusion.1
  707.7 2.3 fusion.3
  712.2 2.2 fusion.9
  714.4 2.2 fusion.12
  726.2 2.4 reshape.243
  733.1 2.1 collective-permute-done.12
  738.9 22.7 %collective-permute-done.14 = f32[2,64,2048]{2,1,0:T(8,128)S(1)} collective-permute-done((f32[2,64,2048]{2,1,0:T(8,128)S(1)}, f32[2,64,2048]{2,1,0:T(8,128)S(1)}, u32[]{:S(2)}, u32[]{:S(2)}) %collective-permute-start.14) | collective-permute-done | bytes 1048608 | tf_op jit(solution)/shard_map/ppermute | solution.py:13
  762.6 21.6 %collective-permute-done.15 = f32[2,64,2048]{2,1,0:T(8,128)} collective-permute-done((f32[2,64,2048]{2,1,0:T(8,128)S(1)}, f32[2,64,2048]{2,1,0:T(8,128)}, u32[]{:S(2)}, u32[]{:S(2)}) %collective-permute-start.15) | collective-permute-done | bytes 1048608 | tf_op jit(solution)/shard_map/ppermute | solution.py:13
  784.2 3.2 add_select_fusion.19
  787.3 2.7 collective-permute-start.16
  790.5 22.1 %collective-permute-done.16 = f32[2,64,2048]{2,1,0:T(8,128)S(1)} collective-permute-done((f32[2,64,2048]{2,1,0:T(8,128)}, f32[2,64,2048]{2,1,0:T(8,128)S(1)}, u32[]{:S(2)}, u32[]{:S(2)}) %collective-permute-start.16) | collective-permute-done | bytes 1048608 | tf_op jit(solution)/shard_map/ppermute | solution.py:13
  813.5 21.6 %collective-permute-done.17 = f32[2,64,2048]{2,1,0:T(8,128)} collective-permute-done((f32[2,64,2048]{2,1,0:T(8,128)S(1)}, f32[2,64,2048]{2,1,0:T(8,128)}, u32[]{:S(2)}, u32[]{:S(2)}) %collective-permute-start.17) | collective-permute-done | bytes 1048608 | tf_op jit(solution)/shard_map/ppermute | solution.py:13
  835.1 2.5 add_select_fusion.17
  837.6 3.2 collective-permute-start.18
  841.3 20.9 %collective-permute-done.18 = f32[2,64,2048]{2,1,0:T(8,128)S(1)} collective-permute-done((f32[2,64,2048]{2,1,0:T(8,128)S(1)}, f32[2,64,2048]{2,1,0:T(8,128)S(1)}, u32[]{:S(2)}, u32[]{:S(2)}) %collective-permute-start.18) | collective-permute-done | bytes 1048608 | tf_op jit(solution)/shard_map/ppermute | solution.py:13
  863.3 21.6 %collective-permute-done.19 = f32[2,64,2048]{2,1,0:T(8,128)} collective-permute-done((f32[2,64,2048]{2,1,0:T(8,128)S(1)}, f32[2,64,2048]{2,1,0:T(8,128)}, u32[]{:S(2)}, u32[]{:S(2)}) %collective-permute-start.19) | collective-permute-done | bytes 1048608 | tf_op jit(solution)/shard_map/ppermute | solution.py:13
  884.9 3.2 add_select_fusion.15
  888.0 3.4 collective-permute-start.20
  891.6 68.0 %collective-permute-done.20 = f32[2,64,2048]{2,1,0:T(8,128)S(1)} collective-permute-done((f32[2,64,2048]{2,1,0:T(8,128)}, f32[2,64,2048]{2,1,0:T(8,128)S(1)}, u32[]{:S(2)}, u32[]{:S(2)}) %collective-permute-start.20) | collective-permute-done | bytes 1048608 | tf_op jit(solution)/shard_map/ppermute | solution.py:13
  960.5 21.6 %collective-permute-done.21 = f32[2,64,2048]{2,1,0:T(8,128)} collective-permute-done((f32[2,64,2048]{2,1,0:T(8,128)S(1)}, f32[2,64,2048]{2,1,0:T(8,128)}, u32[]{:S(2)}, u32[]{:S(2)}) %collective-permute-start.21) | collective-permute-done | bytes 1048608 | tf_op jit(solution)/shard_map/ppermute | solution.py:13
  982.1 2.5 add_select_fusion.13
  984.6 5.4 collective-permute-start.22
  990.3 54.5 %collective-permute-done.22 = f32[2,64,2048]{2,1,0:T(8,128)S(1)} collective-permute-done((f32[2,64,2048]{2,1,0:T(8,128)S(1)}, f32[2,64,2048]{2,1,0:T(8,128)S(1)}, u32[]{:S(2)}, u32[]{:S(2)}) %collective-permute-start.22) | collective-permute-done | bytes 1048608 | tf_op jit(solution)/shard_map/ppermute | solution.py:13
  1044.8 35.4 %collective-permute-done.23 = f32[2,64,2048]{2,1,0:T(8,128)} collective-permute-done((f32[2,64,2048]{2,1,0:T(8,128)S(1)}, f32[2,64,2048]{2,1,0:T(8,128)}, u32[]{:S(2)}, u32[]{:S(2)}) %collective-permute-start.23) | collective-permute-done | bytes 1048608 | tf_op jit(solution)/shard_map/ppermute | solution.py:13
  1083.9 25.3 %all-gather.2.cloned.1.call-done = bf16[256,2048]{1,0:T(8,128)(2,1)} async-done(((bf16[64,2048]{1,0:T(8,128)(2,1)}), bf16[256,2048]{1,0:T(8,128)(2,1)}) %all-gather.2.cloned.1.call-update) | async-done | bytes 1048592 | tf_op jit(solution)/shard_map/all_gather | solution.py:157
  1109.2 2.2 fusion
  (73 shorter events, 47.9 us)
Async XLA Ops:
  6.5 1102.7 %copy-start = (bf16[256,64]{0,1:T(8,128)(2,1)S(1)}, bf16[256,64]{0,1:T(8,128)(2,1)}, u32[]{:S(2)}) copy-start(bf16[256,64]{0,1:T(8,128)(2,1)} %param.11) | copy-start | bytes 98308
  6.5 1102.7 %all-gather.2.cloned.1.call-start = ((), (), s32[]{:S(2)}) async-start(), calls=%async_computation | async-start | bytes 1310720 | tf_op jit(solution)/shard_map/all_gather | solution.py:157
  6.7 2.3 copy-start.4
  10.8 69.0 %collective-permute-start = (f32[2,2,64,2048]{3,2,1,0:T(8,128)}, f32[2,2,64,2048]{3,2,1,0:T(8,128)}, u32[]{:S(2)}, u32[]{:S(2)}) collective-permute-start(f32[2,2,64,2048]{3,2,1,0:T(8,128)} %pad_maximum_fusion), channel_id=1, source_target_pairs={{0,128},{4,132},{8,136},{12,140},{16,144},{20,148},{24,152},{28,15... | collective-permute-start | bytes 6291464 | tf_op jit(solution)/shard_map/ppermute | solution.py:13
  20.1 151.5 %collective-permute-start.1 = (f32[2,2,64,2048]{3,2,1,0:T(8,128)}, f32[2,2,64,2048]{3,2,1,0:T(8,128)}, u32[]{:S(2)}, u32[]{:S(2)}) collective-permute-start(f32[2,2,64,2048]{3,2,1,0:T(8,128)} %stack.34), channel_id=1, source_target_pairs={{0,128},{4,132},{8,136},{12,140},{16,144},{20,148},{24,152},{28,15... | collective-permute-start | bytes 6291464 | tf_op jit(solution)/shard_map/ppermute | solution.py:13
  176.9 163.6 %collective-permute-start.2 = (f32[2,2,64,2048]{3,2,1,0:T(8,128)}, f32[2,2,64,2048]{3,2,1,0:T(8,128)S(1)}, u32[]{:S(2)}, u32[]{:S(2)}) collective-permute-start(f32[2,2,64,2048]{3,2,1,0:T(8,128)} %get-tuple-element.17), channel_id=1, source_target_pairs={{0,64},{4,68},{8,72},{12,76},{16,80},{20,84},{24,88},{28,92},{32,9... | collective-permute-start | bytes 6291464 | tf_op jit(solution)/shard_map/ppermute | solution.py:13
  206.4 179.2 %collective-permute-start.3 = (f32[2,2,64,2048]{3,2,1,0:T(8,128)}, f32[2,2,64,2048]{3,2,1,0:T(8,128)}, u32[]{:S(2)}, u32[]{:S(2)}) collective-permute-start(f32[2,2,64,2048]{3,2,1,0:T(8,128)} %get-tuple-element.16), channel_id=1, source_target_pairs={{0,64},{4,68},{8,72},{12,76},{16,80},{20,84},{24,88},{28,92},{32,9... | collective-permute-start | bytes 6291464 | tf_op jit(solution)/shard_map/ppermute | solution.py:13
  340.5 1.3 copy-start.2
  391.6 47.3 %collective-permute-start.4 = (f32[2,2,64,2048]{3,2,1,0:T(8,128)}, f32[2,2,64,2048]{3,2,1,0:T(8,128)}, u32[]{:S(2)}, u32[]{:S(2)}) collective-permute-start(f32[2,2,64,2048]{3,2,1,0:T(8,128)} %get-tuple-element.15), channel_id=1, source_target_pairs={{0,32},{4,36},{8,40},{12,44},{16,48},{20,52},{24,56},{28,60},{32,0... | collective-permute-start | bytes 6291464 | tf_op jit(solution)/shard_map/ppermute | solution.py:13
  394.0 89.6 %collective-permute-start.5 = (f32[2,2,64,2048]{3,2,1,0:T(8,128)S(1)}, f32[2,2,64,2048]{3,2,1,0:T(8,128)}, u32[]{:S(2)}, u32[]{:S(2)}) collective-permute-start(f32[2,2,64,2048]{3,2,1,0:T(8,128)S(1)} %get-tuple-element.14), channel_id=1, source_target_pairs={{0,32},{4,36},{8,40},{12,44},{16,48},{20,52},{24,56},{28,60},{32,0... | collective-permute-start | bytes 6291464 | tf_op jit(solution)/shard_map/ppermute | solution.py:13
  489.8 46.7 %collective-permute-start.6 = (f32[2,2,64,2048]{3,2,1,0:T(8,128)}, f32[2,2,64,2048]{3,2,1,0:T(8,128)S(1)}, u32[]{:S(2)}, u32[]{:S(2)}) collective-permute-start(f32[2,2,64,2048]{3,2,1,0:T(8,128)} %get-tuple-element.13), channel_id=1, source_target_pairs={{0,16},{4,20},{8,24},{12,28},{16,0},{20,4},{24,8},{28,12},{32,48},... | collective-permute-start | bytes 6291464 | tf_op jit(solution)/shard_map/ppermute | solution.py:13
  492.5 89.0 %collective-permute-start.7 = (f32[2,2,64,2048]{3,2,1,0:T(8,128)}, f32[2,2,64,2048]{3,2,1,0:T(8,128)}, u32[]{:S(2)}, u32[]{:S(2)}) collective-permute-start(f32[2,2,64,2048]{3,2,1,0:T(8,128)} %get-tuple-element.12), channel_id=1, source_target_pairs={{0,16},{4,20},{8,24},{12,28},{16,0},{20,4},{24,8},{28,12},{32,48},... | collective-permute-start | bytes 6291464 | tf_op jit(solution)/shard_map/ppermute | solution.py:13
  536.5 1.3 copy-start.3
  587.5 44.5 %collective-permute-start.8 = (f32[2,2,64,2048]{3,2,1,0:T(8,128)}, f32[2,2,64,2048]{3,2,1,0:T(8,128)}, u32[]{:S(2)}, u32[]{:S(2)}) collective-permute-start(f32[2,2,64,2048]{3,2,1,0:T(8,128)} %get-tuple-element.11), channel_id=1, source_target_pairs={{0,8},{4,12},{8,0},{12,4},{16,24},{20,28},{24,16},{28,20},{32,40},... | collective-permute-start | bytes 6291464 | tf_op jit(solution)/shard_map/ppermute | solution.py:13
  588.8 88.2 %collective-permute-start.9 = (f32[2,2,64,2048]{3,2,1,0:T(8,128)S(1)}, f32[2,2,64,2048]{3,2,1,0:T(8,128)}, u32[]{:S(2)}, u32[]{:S(2)}) collective-permute-start(f32[2,2,64,2048]{3,2,1,0:T(8,128)S(1)} %get-tuple-element.10), channel_id=1, source_target_pairs={{0,8},{4,12},{8,0},{12,4},{16,24},{20,28},{24,16},{28,20},{32,40},... | collective-permute-start | bytes 6291464 | tf_op jit(solution)/shard_map/ppermute | solution.py:13
  683.0 8.2 collective-permute-start.10
  687.3 7.1 collective-permute-start.11
  730.6 1.5 copy-start.1
  732.5 2.7 collective-permute-start.12
  732.9 3.8 collective-permute-start.13
  737.2 24.4 %collective-permute-start.14 = (f32[2,64,2048]{2,1,0:T(8,128)S(1)}, f32[2,64,2048]{2,1,0:T(8,128)S(1)}, u32[]{:S(2)}, u32[]{:S(2)}) collective-permute-start(f32[2,64,2048]{2,1,0:T(8,128)S(1)} %get-tuple-element.27), channel_id=1, source_target_pairs={{0,8},{4,12},{8,0},{12,4},{16,24},{20,28},{24,16},{28,20},{32,40},... | collective-permute-start | bytes 3145736 | tf_op jit(solution)/shard_map/ppermute | solution.py:13
  738.5 45.7 %collective-permute-start.15 = (f32[2,64,2048]{2,1,0:T(8,128)S(1)}, f32[2,64,2048]{2,1,0:T(8,128)}, u32[]{:S(2)}, u32[]{:S(2)}) collective-permute-start(f32[2,64,2048]{2,1,0:T(8,128)S(1)} %get-tuple-element.26), channel_id=1, source_target_pairs={{0,8},{4,12},{8,0},{12,4},{16,24},{20,28},{24,16},{28,20},{32,40},... | collective-permute-start | bytes 3145736 | tf_op jit(solution)/shard_map/ppermute | solution.py:13
  761.6 1.0 copy-start.6
  787.3 25.2 %collective-permute-start.16 = (f32[2,64,2048]{2,1,0:T(8,128)}, f32[2,64,2048]{2,1,0:T(8,128)S(1)}, u32[]{:S(2)}, u32[]{:S(2)}) collective-permute-start(f32[2,64,2048]{2,1,0:T(8,128)} %get-tuple-element.25), channel_id=1, source_target_pairs={{0,16},{4,20},{8,24},{12,28},{16,0},{20,4},{24,8},{28,12},{32,48},... | collective-permute-start | bytes 3145736 | tf_op jit(solution)/shard_map/ppermute | solution.py:13
  790.1 45.0 %collective-permute-start.17 = (f32[2,64,2048]{2,1,0:T(8,128)S(1)}, f32[2,64,2048]{2,1,0:T(8,128)}, u32[]{:S(2)}, u32[]{:S(2)}) collective-permute-start(f32[2,64,2048]{2,1,0:T(8,128)S(1)} %get-tuple-element.24), channel_id=1, source_target_pairs={{0,16},{4,20},{8,24},{12,28},{16,0},{20,4},{24,8},{28,12},{32,48},... | collective-permute-start | bytes 3145736 | tf_op jit(solution)/shard_map/ppermute | solution.py:13
  812.6 1.0 copy-start.7
  837.6 24.7 %collective-permute-start.18 = (f32[2,64,2048]{2,1,0:T(8,128)S(1)}, f32[2,64,2048]{2,1,0:T(8,128)S(1)}, u32[]{:S(2)}, u32[]{:S(2)}) collective-permute-start(f32[2,64,2048]{2,1,0:T(8,128)S(1)} %get-tuple-element.23), channel_id=1, source_target_pairs={{0,32},{4,36},{8,40},{12,44},{16,48},{20,52},{24,56},{28,60},{32,0... | collective-permute-start | bytes 3145736 | tf_op jit(solution)/shard_map/ppermute | solution.py:13
  840.8 44.0 %collective-permute-start.19 = (f32[2,64,2048]{2,1,0:T(8,128)S(1)}, f32[2,64,2048]{2,1,0:T(8,128)}, u32[]{:S(2)}, u32[]{:S(2)}) collective-permute-start(f32[2,64,2048]{2,1,0:T(8,128)S(1)} %get-tuple-element.22), channel_id=1, source_target_pairs={{0,32},{4,36},{8,40},{12,44},{16,48},{20,52},{24,56},{28,60},{32,0... | collective-permute-start | bytes 3145736 | tf_op jit(solution)/shard_map/ppermute | solution.py:13
  862.3 1.0 copy-start.8
  888.0 71.5 %collective-permute-start.20 = (f32[2,64,2048]{2,1,0:T(8,128)}, f32[2,64,2048]{2,1,0:T(8,128)S(1)}, u32[]{:S(2)}, u32[]{:S(2)}) collective-permute-start(f32[2,64,2048]{2,1,0:T(8,128)} %get-tuple-element.21), channel_id=1, source_target_pairs={{0,64},{4,68},{8,72},{12,76},{16,80},{20,84},{24,88},{28,92},{32,9... | collective-permute-start | bytes 3145736 | tf_op jit(solution)/shard_map/ppermute | solution.py:13
  891.4 90.7 %collective-permute-start.21 = (f32[2,64,2048]{2,1,0:T(8,128)S(1)}, f32[2,64,2048]{2,1,0:T(8,128)}, u32[]{:S(2)}, u32[]{:S(2)}) collective-permute-start(f32[2,64,2048]{2,1,0:T(8,128)S(1)} %get-tuple-element.20), channel_id=1, source_target_pairs={{0,64},{4,68},{8,72},{12,76},{16,80},{20,84},{24,88},{28,92},{32,9... | collective-permute-start | bytes 3145736 | tf_op jit(solution)/shard_map/ppermute | solution.py:13
  959.5 1.0 copy-start.9
  984.6 60.2 %collective-permute-start.22 = (f32[2,64,2048]{2,1,0:T(8,128)S(1)}, f32[2,64,2048]{2,1,0:T(8,128)S(1)}, u32[]{:S(2)}, u32[]{:S(2)}) collective-permute-start(f32[2,64,2048]{2,1,0:T(8,128)S(1)} %get-tuple-element.19), channel_id=1, source_target_pairs={{0,128},{4,132},{8,136},{12,140},{16,144},{20,148},{24,152},{28,15... | collective-permute-start | bytes 3145736 | tf_op jit(solution)/shard_map/ppermute | solution.py:13
  990.0 90.2 %collective-permute-start.23 = (f32[2,64,2048]{2,1,0:T(8,128)S(1)}, f32[2,64,2048]{2,1,0:T(8,128)}, u32[]{:S(2)}, u32[]{:S(2)}) collective-permute-start(f32[2,64,2048]{2,1,0:T(8,128)S(1)} %get-tuple-element.18), channel_id=1, source_target_pairs={{0,128},{4,132},{8,136},{12,140},{16,144},{20,148},{24,152},{28,15... | collective-permute-start | bytes 3145736 | tf_op jit(solution)/shard_map/ppermute | solution.py:13
  990.3 91.5 %copy-start.5 = (bf16[64,2048]{1,0:T(8,128)(2,1)S(1)}, bf16[64,2048]{1,0:T(8,128)(2,1)}, u32[]{:S(2)}) copy-start(bf16[64,2048]{1,0:T(8,128)(2,1)} %param.6) | copy-start | bytes 786436
  990.3 91.5 %copy-start.10 = (bf16[64,2048]{1,0:T(8,128)(2,1)S(1)}, bf16[64,2048]{1,0:T(8,128)(2,1)}, u32[]{:S(2)}) copy-start(bf16[64,2048]{1,0:T(8,128)(2,1)} %param.8) | copy-start | bytes 786436
  990.3 91.5 %copy-start.11 = (f32[64]{0:T(128)S(1)}, f32[64]{0:T(128)}, u32[]{:S(2)}) copy-start(f32[64]{0:T(128)} %param.10) | copy-start | bytes 772
Sparse Core Ops, SparseCore 0:
  1084.1 25.1 all-gather.1
where the time goes:
time: 1130 us; the launch traced here: 1120 us
  waiting for transfers between devices  939 us (83%)
  starting transfers between devices  66.1 us (6%)
  other arithmetic  54.8 us (5%)
  matrix products  30.2 us (3%)
  between operations  15.9 us (1%)
  local copies, waits for them, and re-layouts  12.9 us (1%)
    ppermute x24, waiting for transfers between devices, partner(): lax.ppermute(x, axis, [(i, i ^ 1 << bit) for i in range(lax.axis_size(axi...  913 us
    ppermute x24, starting transfers between devices, partner(): lax.ppermute(x, axis, [(i, i ^ 1 << bit) for i in range(lax.axis_size(axi...  66.1 us
    select_n x5, other arithmetic, on_device(): jnp.where(is_lower, delta_imaginary, imaginary + other_imaginary)  29.4 us
    all_gather x1, waiting for transfers between devices, on_device(): lax.all_gather(gated_values, 'ch', axis=0, tiled=True)  25.3 us
  transfers between devices with their start and end apart: 25, of which 25 were waited for; matrix products, arithmetic and copies ran while one was open for 0% of the time, Pallas kernels for 0%

commit v1 on v0

v1 whole, which is shorter than its diff:
```python
import functools
import math

import jax
import jax.numpy as jnp
import ml_dtypes
import numpy as np
from jax import lax
from jax.experimental import pallas as pl
from jax.experimental.pallas import tpu as pltpu
from jax.sharding import PartitionSpec as P

F32 = jnp.float32
BF16 = jnp.bfloat16
MESH = pl.DeviceIdType.MESH

N_CTX = 64
N_CH = 4
CHUNK = 2048
ROWS = 16
T = N_CTX * CHUNK
A = 512
B = 256
GROUP = 16
GROUPS = N_CTX // GROUP
TILE = 256


def split(table):
    table = np.asarray(table, np.float32)
    high = table.astype(ml_dtypes.bfloat16)
    return high, (table - high.astype(np.float32)).astype(ml_dtypes.bfloat16)


@functools.cache
def tables():
    freq = np.arange(A)[:, None] + 0.25
    outer = 2 * np.pi * freq * np.arange(A)[None, :] / A
    outer = np.concatenate([np.cos(outer), -np.sin(outer)], 0)
    turn = 2 * np.pi * freq * np.arange(B)[None, :] / T
    inner = 2 * np.pi * np.outer(np.arange(B), np.arange(B)) / B
    c, s = np.cos(inner), np.sin(inner)
    ahead = np.block([[c, -s], [s, c]])
    back = np.block([[c, s], [-s, c]])
    return (
        split(outer),
        split(outer.T / T),
        split(ahead),
        split(back),
        np.cos(turn).astype(np.float32),
        (-np.sin(turn)).astype(np.float32),
    )


def dot(a, b):
    return jnp.dot(a, b, preferred_element_type=F32)


def parts_of(x):
    high = x.astype(BF16)
    return high, (x - high.astype(F32)).astype(BF16)


def times_right(x, table_hi, table_lo):
    high, low = parts_of(x)
    return dot(high, table_hi[...]) + dot(high, table_lo[...]) + dot(low, table_hi[...])


def sub_row(r):
    return (r % 2) * (ROWS // 2) + r // 2


def chunks_to_matrix(recv):
    x = recv[...].astype(F32)
    half = ROWS // 2
    left = x[:, :half, :].reshape(A, 128)
    right = x[:, half:, :].reshape(A, 128)
    return jnp.concatenate([left, right], axis=1).astype(BF16)


def kernel(
    v_hbm, k_hbm, q_hbm, f_hbm, skip_hbm, w_hbm,
    oh_hbm, ol_hbm, ph_hbm, pl_hbm, ah_hbm, al_hbm, bh_hbm, bl_hbm, tc_hbm, ts_hbm,
    out_ref,
    v_ref, k_ref, q_ref, f_ref, skip_row, w_ref,
    oh, ol, ph, plo, ah, al, bh, bl, tc, ts,
    stage, send_s, send_f, send_y, recv_s, recv_f, recv_y,
    skip_ref, x_ref, spec, y_hi, y_lo, conv32, gathered,
    in_sem, table_sem, s_send, s_recv, f_send, f_recv, y_send, y_recv, g_send, g_recv,
):
    me = lax.axis_index("ctx")
    ch = lax.axis_index("ch")

    loads = [
        pltpu.make_async_copy(src, dst, in_sem.at[i])
        for i, (src, dst) in enumerate(
            [(v_hbm, v_ref), (k_hbm, k_ref), (f_hbm, f_ref), (q_hbm, q_ref), (skip_hbm, skip_row), (w_hbm, w_ref)]
        )
    ]
    table_loads = [
        pltpu.make_async_copy(src, dst, table_sem.at[i])
        for i, (src, dst) in enumerate(
            [
                (oh_hbm, oh), (ol_hbm, ol), (tc_hbm, tc), (ts_hbm, ts), (ah_hbm, ah), (al_hbm, al),
                (bh_hbm, bh), (bl_hbm, bl), (ph_hbm, ph), (pl_hbm, plo),
            ]
        )
    ]
    for copy in loads + table_loads:
        copy.start()

    barrier = pltpu.get_barrier_semaphore()

    def greet(o, carry):
        peer = lax.rem(me + o, N_CTX)
        pl.semaphore_signal(barrier, inc=1, device_id=(peer, ch), device_id_type=MESH)
        return carry

    lax.fori_loop(1, N_CTX, greet, 0)
    for o in range(1, N_CH):
        pl.semaphore_signal(barrier, inc=1, device_id=(me, lax.rem(ch + o, N_CH)), device_id_type=MESH)

    def to_chunks(value, send):
        for r in range(ROWS):
            stage[pl.ds(sub_row(r), N_CTX, stride=ROWS), :] = value(r)
        send[...] = stage[...].astype(BF16).reshape(N_CTX, ROWS, 128)

    def tile(ref, r):
        return ref[:, r * 128 : (r + 1) * 128].astype(F32)

    loads[0].wait()
    loads[1].wait()
    to_chunks(lambda r: tile(v_ref, r) * tile(k_ref, r), send_s)
    loads[2].wait()
    to_chunks(lambda r: tile(f_ref, r), send_f)

    pl.semaphore_wait(barrier, N_CTX - 1 + N_CH - 1)

    def chunk_copy(send, recv, s_sem, r_sem, peer):
        return pltpu.make_async_remote_copy(
            src_ref=send.at[peer], dst_ref=recv.at[me], send_sem=s_sem, recv_sem=r_sem,
            device_id=(peer, ch), device_id_type=MESH,
        )

    def scatter(send, recv, s_sem, r_sem):
        pltpu.make_async_copy(send.at[me], recv.at[me], r_sem).start()

        def step(o, carry):
            chunk_copy(send, recv, s_sem, r_sem, lax.rem(me + o, N_CTX)).start()
            return carry

        lax.fori_loop(1, N_CTX, step, 0)

    def whole(ref, s_sem, r_sem):
        return pltpu.make_async_remote_copy(
            src_ref=ref, dst_ref=ref, send_sem=s_sem, recv_sem=r_sem,
            device_id=(lax.rem(me + 1, N_CTX), ch), device_id_type=MESH,
        )

    scatter(send_s, recv_s, s_send, s_recv)
    scatter(send_f, recv_f, f_send, f_recv)

    for copy in table_loads:
        copy.wait()

    def forward(row):
        x = x_ref[...]
        up, down = pl.ds(row, TILE), pl.ds(A + row, TILE)
        re = dot(oh[up, :], x) + dot(ol[up, :], x)
        im = dot(oh[down, :], x) + dot(ol[down, :], x)
        c, s = tc[up, :], ts[up, :]
        return times_right(jnp.concatenate([re * c - im * s, re * s + im * c], axis=1), ah, al)

    whole(recv_s, s_send, s_recv).wait_recv()
    x_ref[...] = chunks_to_matrix(recv_s)

    def signal_step(i, carry):
        row = pl.multiple_of(i * TILE, TILE)
        spec[pl.ds(row, TILE), :] = forward(row)
        return carry

    lax.fori_loop(0, A // TILE, signal_step, 0)

    whole(recv_f, f_send, f_recv).wait_recv()
    x_ref[...] = chunks_to_matrix(recv_f)

    def taps_step(i, carry):
        row = pl.multiple_of(i * TILE, TILE)
        up, down = pl.ds(row, TILE), pl.ds(A + row, TILE)
        taps = forward(row)
        fr, fi = taps[:, :B], taps[:, B:]
        sr, si = spec[up, :B], spec[up, B:]
        product = jnp.concatenate([sr * fr - si * fi, sr * fi + si * fr], axis=1)
        y = times_right(product, bh, bl)
        re, im = y[:, :B], y[:, B:]
        c, s = tc[up, :], ts[up, :]
        re, im = re * c + im * s, im * c - re * s
        y_hi[up, :], y_lo[up, :] = parts_of(re)
        y_hi[down, :], y_lo[down, :] = parts_of(im)
        return carry

    lax.fori_loop(0, A // TILE, taps_step, 0)

    per_group = A // GROUPS
    mine = me // GROUP

    def inverse_step(i, carry):
        g = lax.rem(mine + i, GROUPS)
        rows = pl.ds(pl.multiple_of(g * per_group, per_group), per_group)
        y = dot(ph[rows, :], y_hi[...]) + dot(plo[rows, :], y_hi[...]) + dot(ph[rows, :], y_lo[...])
        half = ROWS // 2
        y = jnp.concatenate(
            [y[:, :128].reshape(GROUP, half, 128), y[:, 128:].reshape(GROUP, half, 128)], axis=1
        )
        send_y[pl.ds(g * GROUP, GROUP)] = y.astype(BF16)

        def step(o, carry):
            peer = g * GROUP + lax.rem(me + o, GROUP)

            @pl.when(peer != me)
            def _():
                chunk_copy(send_y, recv_y, y_send, y_recv.at[mine], peer).start()

            @pl.when(peer == me)
            def _():
                pltpu.make_async_copy(send_y.at[me], recv_y.at[me], y_recv.at[mine]).start()

            return carry

        return lax.fori_loop(0, GROUP, step, carry)

    lax.fori_loop(0, GROUPS, inverse_step, 0)

    for copy in loads[3:]:
        copy.wait()
    eye = lax.broadcasted_iota(jnp.int32, (N_CTX, N_CTX), 0) == lax.broadcasted_iota(jnp.int32, (N_CTX, N_CTX), 1)
    skip_ref[...] = jnp.where(eye, skip_row[...], 0.0)

    def gate_copy(rows, o):
        return pltpu.make_async_remote_copy(
            src_ref=gathered.at[ch, rows], dst_ref=gathered.at[ch, rows],
            send_sem=g_send, recv_sem=g_recv,
            device_id=(me, lax.rem(ch + o, N_CH)), device_id_type=MESH,
        )

    for g in range(GROUPS):
        rows = slice(g * GROUP, (g + 1) * GROUP)
        whole(recv_y.at[rows], y_send, y_recv.at[g]).wait_recv()
        conv32[...] = recv_y[rows].astype(F32).reshape(GROUP * ROWS, 128)
        gain = jnp.sum(skip_ref[rows, :], axis=1, keepdims=True)
        for r in range(ROWS):
            lanes = slice(r * 128, (r + 1) * 128)
            c = conv32[pl.ds(sub_row(r), GROUP, stride=ROWS), :]
            gated = q_ref[rows, lanes].astype(F32) * (c + gain * v_ref[rows, lanes].astype(F32))
            gathered[ch, rows, lanes] = gated.astype(BF16)
        for o in (2, 1, 3):
            gate_copy(pl.ds(g * GROUP, GROUP), o).start()

    three = gathered.at[pl.ds(0, N_CH - 1)]
    done = pltpu.make_async_remote_copy(
        src_ref=three, dst_ref=three, send_sem=g_send, recv_sem=g_recv,
        device_id=(me, lax.rem(ch + 1, N_CH)), device_id_type=MESH,
    )
    done.wait_recv()
    for r in range(CHUNK // 512):
        lanes = slice(r * 512, (r + 1) * 512)
        mixed = lax.dot_general(
            w_ref[...], gathered[:, :, lanes].reshape(N_CH * N_CTX, 512),
            (((0,), (0,)), ((), ())), preferred_element_type=F32,
        )
        out_ref[:, lanes] = mixed.astype(BF16)

    done.wait_send()
    most = pl.ds(0, N_CTX - 1)
    whole(send_s.at[most], s_send, s_recv).wait_send()
    whole(send_f.at[most], f_send, f_recv).wait_send()
    whole(send_y.at[most], y_send, y_recv.at[0]).wait_send()


def on_device(value_in, key_gate, query_gate, filter_taps, skip_gain, out_weight):
    (oh, ol), (ph, plo), (ah, al), (bh, bl), tc, ts = tables()
    consts = [oh, ol, ph, plo, ah, al, bh, bl, tc, ts]
    args = [value_in, key_gate, query_gate, filter_taps, skip_gain.reshape(1, N_CTX), out_weight]
    args += [jnp.asarray(c) for c in consts]
    vm = pltpu.VMEM
    copies = [vm((N_CTX, CHUNK), BF16)] * 3 + [vm((N_CTX, CHUNK), F32), vm((1, N_CTX), F32), vm((N_CH * N_CTX, N_CTX), BF16)]
    copies += [vm(c.shape, c.dtype) for c in consts]
    chunk = vm((N_CTX, ROWS, 128), BF16)
    dma = pltpu.SemaphoreType.DMA
    return pl.pallas_call(
        kernel,
        out_shape=jax.ShapeDtypeStruct((N_CTX, CHUNK), BF16),
        in_specs=[pl.BlockSpec(memory_space=pl.ANY)] * len(args),
        out_specs=pl.BlockSpec(memory_space=pltpu.VMEM),
        scratch_shapes=copies
        + [vm((N_CTX * ROWS, 128), F32)]
        + [chunk] * 6
        + [
            vm((N_CTX, N_CTX), F32),
            vm((A, B), BF16),
            vm((A, 2 * B), F32),
            vm((2 * A, B), BF16),
            vm((2 * A, B), BF16),
            vm((GROUP * ROWS, 128), F32),
            vm((N_CH, N_CTX, CHUNK), BF16),
            dma((6,)), dma((10,)), dma, dma, dma, dma, dma, dma((GROUPS,)), dma, dma,
        ],
        compiler_params=pltpu.CompilerParams(
            collective_id=0, has_side_effects=True, vmem_limit_bytes=48 * 1024 * 1024
        ),
        name="hyena",
    )(*args)


def solution(mesh):
    placed = (
        P("ch", "ctx"),
        P("ch", "ctx"),
        P("ch", "ctx"),
        P("ch", "ctx"),
        P("ch"),
        P(None, "ch"),
    )
    return jax.shard_map(
        on_device, mesh=mesh, in_specs=placed, out_specs=P("ch", "ctx"), check_vma=False
    )
```

time: 1130 us -> 66.5 us (0.06)
  waiting for transfers between devices: 939 us -> 0 us
  starting transfers between devices: 66.1 us -> 0 us
  other arithmetic: 54.8 us -> 0 us
  Pallas kernels: 0 us -> 52.9 us
  matrix products: 30.2 us -> 0 us
  between operations: 15.9 us -> 0.04 us
    ppermute x24 -> x0, waiting for transfers between devices: 913 us -> none  [partner(): lax.ppermute(x, axis, [(i, i ^ 1 << bit) for i in range(lax.axis_size(axi...]
    ppermute x24 -> x0, starting transfers between devices: 66.1 us -> none  [partner(): lax.ppermute(x, axis, [(i, i ^ 1 << bit) for i in range(lax.axis_size(axi...]
    pallas_call x0 -> x1, Pallas kernels: none -> 52.9 us  [on_device(): pl.pallas_call(kernel, out_shape=jax.ShapeDtypeStruct((N_CTX, CHUNK), BF1...]
    select_n x11 -> x0, other arithmetic: 42.8 us -> none  [the longest x5 29.4 us: on_device(): jnp.where(is_lower, delta_imaginary, imaginary + other_imaginary)]
    dot_general x17 -> x0, matrix products: 30.2 us -> none  [the longest x8 14 us: multiply(): return jnp.einsum('...ab,ak->...kb', operand, table, precision=PRECISE)]
    all_gather x1 -> x0, waiting for transfers between devices: 25.3 us -> none  [on_device(): lax.all_gather(gated_values, 'ch', axis=0, tiled=True)]
  transfers between devices with their start and end apart: 25 -> 0, of which waited for: 25 -> 0; matrix products, arithmetic and copies ran while one was open for 0% -> 0% of each run, Pallas kernels for 0% -> 0%
where the time goes in v1:
time: 66.5 us; the launch traced here: 65.9 us
  Pallas kernels  52.9 us (80%)
  local copies, waits for them, and re-layouts  12.9 us (19%)
    pallas_call x1, Pallas kernels, on_device(): pl.pallas_call(kernel, out_shape=jax.ShapeDtypeStruct((N_CTX, CHUNK), BF1...  52.9 us
    unnamed x26, local copies, waits for them, and re-layouts  12.9 us

profile of v1, /device:TPU:1, one launch (start us, length us, event | category | flops | bytes accessed | tf_op | source)
XLA Modules:
  0.0 65.9 jit_solution(13215245564873147863)
XLA Ops:
  0.0 0.0 copy-start.11
  0.0 0.9 %copy.17.w_hbm = bf16[256,64]{1,0:T(8,128)(2,1)S(1)} copy(bf16[256,64]{0,1:T(8,128)(2,1)} %param.21) | data formatting | bytes 65536 | tf_op args[5]
  0.9 0.0 copy-done.11
  0.9 0.0 copy-start
  0.9 1.2 %copy-done = bf16[1024,512]{1,0:T(8,128)(2,1)S(1)} copy-done((bf16[1024,512]{1,0:T(8,128)(2,1)S(1)}, bf16[1024,512]{1,0:T(8,128)(2,1)}, u32[]{:S(2)}) %copy-start) | copy-done | bytes 1048600
  2.1 0.0 copy-start.1
  2.1 1.0 %copy-done.1 = f32[64,2048]{1,0:T(8,128)S(1)} copy-done((f32[64,2048]{1,0:T(8,128)S(1)}, f32[64,2048]{1,0:T(8,128)}, u32[]{:S(2)}) %copy-start.1) | copy-done | bytes 524312
  3.2 0.0 copy-start.2
  3.2 1.0 %copy-done.2 = f32[512,256]{1,0:T(8,128)S(1)} copy-done((f32[512,256]{1,0:T(8,128)S(1)}, f32[512,256]{1,0:T(8,128)}, u32[]{:S(2)}) %copy-start.2) | copy-done | bytes 524312
  4.2 0.0 copy-start.3
  4.2 1.0 %copy-done.3 = f32[512,256]{1,0:T(8,128)S(1)} copy-done((f32[512,256]{1,0:T(8,128)S(1)}, f32[512,256]{1,0:T(8,128)}, u32[]{:S(2)}) %copy-start.3) | copy-done | bytes 524312
  5.3 0.0 copy-start.4
  5.3 1.0 %copy-done.4 = bf16[512,512]{1,0:T(8,128)(2,1)S(1)} copy-done((bf16[512,512]{1,0:T(8,128)(2,1)S(1)}, bf16[512,512]{1,0:T(8,128)(2,1)}, u32[]{:S(2)}) %copy-start.4) | copy-done | bytes 524312
  6.3 0.0 copy-start.5
  6.3 1.0 %copy-done.5 = bf16[512,512]{1,0:T(8,128)(2,1)S(1)} copy-done((bf16[512,512]{1,0:T(8,128)(2,1)S(1)}, bf16[512,512]{1,0:T(8,128)(2,1)}, u32[]{:S(2)}) %copy-start.5) | copy-done | bytes 524312
  7.3 0.0 copy-start.6
  7.3 1.0 %copy-done.6 = bf16[512,512]{1,0:T(8,128)(2,1)S(1)} copy-done((bf16[512,512]{1,0:T(8,128)(2,1)S(1)}, bf16[512,512]{1,0:T(8,128)(2,1)}, u32[]{:S(2)}) %copy-start.6) | copy-done | bytes 524312
  8.4 0.0 copy-start.7
  8.4 1.0 %copy-done.7 = bf16[512,512]{1,0:T(8,128)(2,1)S(1)} copy-done((bf16[512,512]{1,0:T(8,128)(2,1)S(1)}, bf16[512,512]{1,0:T(8,128)(2,1)}, u32[]{:S(2)}) %copy-start.7) | copy-done | bytes 524312
  9.4 0.0 copy-start.8
  9.4 0.9 %copy-done.8 = bf16[64,2048]{1,0:T(8,128)(2,1)S(1)} copy-done((bf16[64,2048]{1,0:T(8,128)(2,1)S(1)}, bf16[64,2048]{1,0:T(8,128)(2,1)}, u32[]{:S(2)}) %copy-start.8) | copy-done | bytes 262168
  10.4 0.0 copy-start.9
  10.4 0.9 %copy-done.9 = bf16[64,2048]{1,0:T(8,128)(2,1)S(1)} copy-done((bf16[64,2048]{1,0:T(8,128)(2,1)S(1)}, bf16[64,2048]{1,0:T(8,128)(2,1)}, u32[]{:S(2)}) %copy-start.9) | copy-done | bytes 262168
  11.3 0.0 copy-start.10
  11.3 0.9 %copy-done.10 = bf16[64,2048]{1,0:T(8,128)(2,1)S(1)} copy-done((bf16[64,2048]{1,0:T(8,128)(2,1)S(1)}, bf16[64,2048]{1,0:T(8,128)(2,1)}, u32[]{:S(2)}) %copy-start.10) | copy-done | bytes 262168
  12.3 52.9 %hyena.1 = bf16[64,2048]{1,0:T(8,128)(2,1)S(1)} custom-call(bf16[64,2048]{1,0:T(8,128)(2,1)S(1)} %copy-done.8, bf16[64,2048]{1,0:T(8,128)(2,1)S(1)} %copy-done.9, bf16[64,2048]{1,0:T(8,128)(2,1)S(1)} %copy-done.10, f32[64,2048]{1,0:T(8,128)S(1)} %copy-done.1, f32[1,64]{1,0:T(1,128)S(1)} %bitcast.1, bf16[256,64]{1,0:T(8,128)(2,1)S(1)} %copy.17.w_hbm, ...), custom_call_target="tpu_custom_call" | custom-call | tf_op jit(solution)/shard_map/hyena/pallas_call | solution.py:290
  65.1 0.7 %copy.19 = bf16[64,2048]{1,0:T(8,128)(2,1)} copy(bf16[64,2048]{1,0:T(8,128)(2,1)S(1)} %hyena.1) | data formatting | bytes 524288
Async XLA Ops:
  0.0 0.9 %copy-start.11 = (f32[64]{0:T(128)S(1)}, f32[64]{0:T(128)}, u32[]{:S(2)}) copy-start(f32[64]{0:T(128)} %param.20) | copy-start | bytes 772
  0.9 1.2 %copy-start = (bf16[1024,512]{1,0:T(8,128)(2,1)S(1)}, bf16[1024,512]{1,0:T(8,128)(2,1)}, u32[]{:S(2)}) copy-start(bf16[1024,512]{1,0:T(8,128)(2,1)} %constant.20.clone.oh_hbm) | copy-start | bytes 3145732
  2.1 1.0 %copy-start.1 = (f32[64,2048]{1,0:T(8,128)S(1)}, f32[64,2048]{1,0:T(8,128)}, u32[]{:S(2)}) copy-start(f32[64,2048]{1,0:T(8,128)} %f_hbm.1) | copy-start | bytes 1572868
  3.2 1.0 %copy-start.2 = (f32[512,256]{1,0:T(8,128)S(1)}, f32[512,256]{1,0:T(8,128)}, u32[]{:S(2)}) copy-start(f32[512,256]{1,0:T(8,128)} %constant.29.clone.ts_hbm) | copy-start | bytes 1572868
  4.2 1.0 %copy-start.3 = (f32[512,256]{1,0:T(8,128)S(1)}, f32[512,256]{1,0:T(8,128)}, u32[]{:S(2)}) copy-start(f32[512,256]{1,0:T(8,128)} %constant.28.clone.tc_hbm) | copy-start | bytes 1572868
  5.3 1.0 %copy-start.4 = (bf16[512,512]{1,0:T(8,128)(2,1)S(1)}, bf16[512,512]{1,0:T(8,128)(2,1)}, u32[]{:S(2)}) copy-start(bf16[512,512]{1,0:T(8,128)(2,1)} %constant.27.clone.bl_hbm) | copy-start | bytes 1572868
  6.3 1.0 %copy-start.5 = (bf16[512,512]{1,0:T(8,128)(2,1)S(1)}, bf16[512,512]{1,0:T(8,128)(2,1)}, u32[]{:S(2)}) copy-start(bf16[512,512]{1,0:T(8,128)(2,1)} %constant.26.clone.bh_hbm) | copy-start | bytes 1572868
  7.3 1.0 %copy-start.6 = (bf16[512,512]{1,0:T(8,128)(2,1)S(1)}, bf16[512,512]{1,0:T(8,128)(2,1)}, u32[]{:S(2)}) copy-start(bf16[512,512]{1,0:T(8,128)(2,1)} %constant.25.clone.al_hbm) | copy-start | bytes 1572868
  8.4 1.0 %copy-start.7 = (bf16[512,512]{1,0:T(8,128)(2,1)S(1)}, bf16[512,512]{1,0:T(8,128)(2,1)}, u32[]{:S(2)}) copy-start(bf16[512,512]{1,0:T(8,128)(2,1)} %constant.24.clone.ah_hbm) | copy-start | bytes 1572868
  9.4 0.9 %copy-start.8 = (bf16[64,2048]{1,0:T(8,128)(2,1)S(1)}, bf16[64,2048]{1,0:T(8,128)(2,1)}, u32[]{:S(2)}) copy-start(bf16[64,2048]{1,0:T(8,128)(2,1)} %v_hbm.1) | copy-start | bytes 786436
  10.4 0.9 %copy-start.9 = (bf16[64,2048]{1,0:T(8,128)(2,1)S(1)}, bf16[64,2048]{1,0:T(8,128)(2,1)}, u32[]{:S(2)}) copy-start(bf16[64,2048]{1,0:T(8,128)(2,1)} %k_hbm.1) | copy-start | bytes 786436
  11.3 0.9 %copy-start.10 = (bf16[64,2048]{1,0:T(8,128)(2,1)S(1)}, bf16[64,2048]{1,0:T(8,128)(2,1)}, u32[]{:S(2)}) copy-start(bf16[64,2048]{1,0:T(8,128)(2,1)} %q_hbm.1) | copy-start | bytes 786436

commit v2 on v1

--- a/solution.py
+++ b/solution.py
@@ -1,9 +1,7 @@
 import functools
-import math
 
 import jax
 import jax.numpy as jnp
-import ml_dtypes
 import numpy as np
 from jax import lax
 from jax.experimental import pallas as pl
@@ -26,29 +24,20 @@
 TILE = 256
 
 
-def split(table):
-    table = np.asarray(table, np.float32)
-    high = table.astype(ml_dtypes.bfloat16)
-    return high, (table - high.astype(np.float32)).astype(ml_dtypes.bfloat16)
+def turns(rows, columns):
+    angle = 2 * np.pi * np.outer(rows, columns)
+    return np.stack([np.cos(angle), np.sin(angle)]).astype(np.float32)
 
 
 @functools.cache
 def tables():
-    freq = np.arange(A)[:, None] + 0.25
-    outer = 2 * np.pi * freq * np.arange(A)[None, :] / A
-    outer = np.concatenate([np.cos(outer), -np.sin(outer)], 0)
-    turn = 2 * np.pi * freq * np.arange(B)[None, :] / T
-    inner = 2 * np.pi * np.outer(np.arange(B), np.arange(B)) / B
-    c, s = np.cos(inner), np.sin(inner)
-    ahead = np.block([[c, -s], [s, c]])
-    back = np.block([[c, s], [-s, c]])
+    coarse, fine = 16 * np.arange(A // 16), np.arange(16)
+    column = np.arange(A)
     return (
-        split(outer),
-        split(outer.T / T),
-        split(ahead),
-        split(back),
-        np.cos(turn).astype(np.float32),
-        (-np.sin(turn)).astype(np.float32),
+        turns(coarse, column / A), turns(fine + 0.25, column / A),
+        turns(coarse, (column + 0.25) / A), turns(fine, (column + 0.25) / A),
+        turns(coarse[: B // 16], np.arange(B) / B), turns(fine, np.arange(B) / B),
+        turns(coarse, np.arange(B) / T), turns(fine + 0.25, np.arange(B) / T),
     )
 
 
@@ -80,9 +69,10 @@
 
 def kernel(
     v_hbm, k_hbm, q_hbm, f_hbm, skip_hbm, w_hbm,
-    oh_hbm, ol_hbm, ph_hbm, pl_hbm, ah_hbm, al_hbm, bh_hbm, bl_hbm, tc_hbm, ts_hbm,
+    fa_hbm, fb_hbm, ga_hbm, gb_hbm, ia_hbm, ib_hbm, ta_hbm, tb_hbm,
     out_ref,
     v_ref, k_ref, q_ref, f_ref, skip_row, w_ref,
+    fa, fb, ga, gb, ia, ib, ta, tb,
     oh, ol, ph, plo, ah, al, bh, bl, tc, ts,
     stage, send_s, send_f, send_y, recv_s, recv_f, recv_y,
     skip_ref, x_ref, spec, y_hi, y_lo, conv32, gathered,
@@ -100,10 +90,10 @@
     table_loads = [
         pltpu.make_async_copy(src, dst, table_sem.at[i])
         for i, (src, dst) in enumerate(
-            [
-                (oh_hbm, oh), (ol_hbm, ol), (tc_hbm, tc), (ts_hbm, ts), (ah_hbm, ah), (al_hbm, al),
-                (bh_hbm, bh), (bl_hbm, bl), (ph_hbm, ph), (pl_hbm, plo),
-            ]
+            zip(
+                (fa_hbm, fb_hbm, ga_hbm, gb_hbm, ia_hbm, ib_hbm, ta_hbm, tb_hbm),
+                (fa, fb, ga, gb, ia, ib, ta, tb),
+            )
         )
     ]
     for copy in loads + table_loads:
@@ -162,6 +152,47 @@
 
     for copy in table_loads:
         copy.wait()
+
+    def block(coarse, fine, i):
+        ca, sa = coarse[0, pl.ds(i, 1), :], coarse[1, pl.ds(i, 1), :]
+        cb, sb = fine[0], fine[1]
+        return ca * cb - sa * sb, ca * sb + sa * cb
+
+    def put(high_ref, low_ref, at, value):
+        high_ref[at], low_ref[at] = parts_of(value)
+
+    def make_outer(i, carry):
+        up = pl.ds(pl.multiple_of(i * 16, 16), 16)
+        down = pl.ds(pl.multiple_of(A + i * 16, 16), 16)
+        c, s = block(fa, fb, i)
+        put(oh, ol, (up,), c)
+        put(oh, ol, (down,), -s)
+        c, s = block(ta, tb, i)
+        tc[up, :], ts[up, :] = c, -s
+        return carry
+
+    def make_inner(i, carry):
+        up = pl.ds(pl.multiple_of(i * 16, 16), 16)
+        down = pl.ds(pl.multiple_of(B + i * 16, 16), 16)
+        left, right = slice(0, B), slice(B, 2 * B)
+        c, s = block(ia, ib, i)
+        for high, low, sign in ((ah, al, 1.0), (bh, bl, -1.0)):
+            put(high, low, (up, left), c)
+            put(high, low, (down, right), c)
+            put(high, low, (up, right), -sign * s)
+            put(high, low, (down, left), sign * s)
+        return carry
+
+    def make_last(i, carry):
+        up = pl.ds(pl.multiple_of(i * 16, 16), 16)
+        c, s = block(ga, gb, i)
+        put(ph, plo, (up, slice(0, A)), c * (1.0 / T))
+        put(ph, plo, (up, slice(A, 2 * A)), s * (-1.0 / T))
+        return carry
+
+    lax.fori_loop(0, A // 16, make_outer, 0)
+    lax.fori_loop(0, B // 16, make_inner, 0)
+    lax.fori_loop(0, A // 16, make_last, 0)
 
     def forward(row):
         x = x_ref[...]
@@ -264,10 +295,7 @@
     done.wait_recv()
     for r in range(CHUNK // 512):
         lanes = slice(r * 512, (r + 1) * 512)
-        mixed = lax.dot_general(
-            w_ref[...], gathered[:, :, lanes].reshape(N_CH * N_CTX, 512),
-            (((0,), (0,)), ((), ())), preferred_element_type=F32,
-        )
+        mixed = dot(w_ref[...], gathered[:, :, lanes].reshape(N_CH * N_CTX, 512))
         out_ref[:, lanes] = mixed.astype(BF16)
 
     done.wait_send()
@@ -278,19 +306,19 @@
 
 
 def on_device(value_in, key_gate, query_gate, filter_taps, skip_gain, out_weight):
-    (oh, ol), (ph, plo), (ah, al), (bh, bl), tc, ts = tables()
-    consts = [oh, ol, ph, plo, ah, al, bh, bl, tc, ts]
-    args = [value_in, key_gate, query_gate, filter_taps, skip_gain.reshape(1, N_CTX), out_weight]
+    consts = tables()
+    args = [value_in, key_gate, query_gate, filter_taps, skip_gain.reshape(1, N_CTX), out_weight.T]
     args += [jnp.asarray(c) for c in consts]
     vm = pltpu.VMEM
-    copies = [vm((N_CTX, CHUNK), BF16)] * 3 + [vm((N_CTX, CHUNK), F32), vm((1, N_CTX), F32), vm((N_CH * N_CTX, N_CTX), BF16)]
+    copies = [vm((N_CTX, CHUNK), BF16)] * 3 + [vm((N_CTX, CHUNK), F32), vm((1, N_CTX), F32), vm((N_CTX, N_CH * N_CTX), BF16)]
     copies += [vm(c.shape, c.dtype) for c in consts]
+    copies += [vm((2 * A, A), BF16)] * 2 + [vm((A, 2 * A), BF16)] * 2 + [vm((2 * B, 2 * B), BF16)] * 4 + [vm((A, B), F32)] * 2
     chunk = vm((N_CTX, ROWS, 128), BF16)
     dma = pltpu.SemaphoreType.DMA
     return pl.pallas_call(
         kernel,
         out_shape=jax.ShapeDtypeStruct((N_CTX, CHUNK), BF16),
-        in_specs=[pl.BlockSpec(memory_space=pl.ANY)] * len(args),
+        in_specs=[pl.BlockSpec(memory_space=pltpu.HBM)] * len(args),
         out_specs=pl.BlockSpec(memory_space=pltpu.VMEM),
         scratch_shapes=copies
         + [vm((N_CTX * ROWS, 128), F32)]
@@ -303,10 +331,10 @@
             vm((2 * A, B), BF16),
             vm((GROUP * ROWS, 128), F32),
             vm((N_CH, N_CTX, CHUNK), BF16),
-            dma((6,)), dma((10,)), dma, dma, dma, dma, dma, dma((GROUPS,)), dma, dma,
+            dma((6,)), dma((8,)), dma, dma, dma, dma, dma, dma((GROUPS,)), dma, dma,
         ],
         compiler_params=pltpu.CompilerParams(
-            collective_id=0, has_side_effects=True, vmem_limit_bytes=48 * 1024 * 1024
+            collective_id=0, has_side_effects=True, vmem_limit_bytes=56 * 1024 * 1024
         ),
         name="hyena",
     )(*args)

time: 66.5 us -> 54.8 us (0.82)
  local copies, waits for them, and re-layouts: 12.9 us -> 1.67 us
    unnamed x26 -> x1, local copies, waits for them, and re-layouts: 12.9 us -> 1.67 us
where the time goes in v2:
time: 54.8 us; the launch traced here: 54.7 us
  Pallas kernels  53 us (97%)
  local copies, waits for them, and re-layouts  1.67 us (3%)
    pallas_call x1, Pallas kernels, on_device(): pl.pallas_call(kernel, out_shape=jax.ShapeDtypeStruct((N_CTX, CHUNK), BF1...  53 us
    unnamed x1, local copies, waits for them, and re-layouts  1.67 us

profile of v2, /device:TPU:1, one launch (start us, length us, event | category | flops | bytes accessed | tf_op | source)
XLA Modules:
  0.0 54.7 jit_solution(6788736745585680515)
XLA Ops:
  0.0 53.0 %hyena.1 = bf16[64,2048]{1,0:T(8,128)(2,1)} custom-call(bf16[64,2048]{1,0:T(8,128)(2,1)} %v_hbm.1, bf16[64,2048]{1,0:T(8,128)(2,1)} %k_hbm.1, bf16[64,2048]{1,0:T(8,128)(2,1)} %q_hbm.1, f32[64,2048]{1,0:T(8,128)} %f_hbm.1, f32[1,64]{1,0:T(1,128)} %bitcast.3, bf16[64,256]{1,0:T(8,128)(2,1)} %bitcast.2, f32[2,32,512]{2,1,0:T(8,128)} %constant.16.clone.fa_hbm, ...), custom_call_target="tpu_custom_call" | custom-call | tf_op jit(solution)/shard_map/hyena/pallas_call | solution.py:318
  53.1 1.7 %copy.16 = bf16[64,2048]{1,0:T(8,128)(2,1)} copy(bf16[64,2048]{1,0:T(8,128)(2,1)} %hyena.1) | data formatting | bytes 524288

commit v3 on v2

--- a/solution.py
+++ b/solution.py
@@ -21,6 +21,7 @@
 B = 256
 GROUP = 16
 GROUPS = N_CTX // GROUP
+PIECES = ROWS // N_CH
 TILE = 256
 
 
@@ -59,6 +60,10 @@
     return (r % 2) * (ROWS // 2) + r // 2
 
 
+def lane_tile(y, i):
+    return 8 * (y % 2) + 2 * i + y // 2
+
+
 def chunks_to_matrix(recv):
     x = recv[...].astype(F32)
     half = ROWS // 2
@@ -71,12 +76,13 @@
     v_hbm, k_hbm, q_hbm, f_hbm, skip_hbm, w_hbm,
     fa_hbm, fb_hbm, ga_hbm, gb_hbm, ia_hbm, ib_hbm, ta_hbm, tb_hbm,
     out_ref,
-    v_ref, k_ref, q_ref, f_ref, skip_row, w_ref,
+    v_ref, k_ref, q_ref, f_ref, skip_row, w_ref, skip_all, w_all,
     fa, fb, ga, gb, ia, ib, ta, tb,
     oh, ol, ph, plo, ah, al, bh, bl, tc, ts,
     stage, send_s, send_f, send_y, recv_s, recv_f, recv_y,
-    skip_ref, x_ref, spec, y_hi, y_lo, conv32, gathered,
-    in_sem, table_sem, s_send, s_recv, f_send, f_recv, y_send, y_recv, g_send, g_recv,
+    side_out, side_in, gain_v, x_ref, spec, y_hi, y_lo, conv32, gated, mix_out, mix_in,
+    in_sem, table_sem, s_send, s_recv, f_send, f_recv, y_send, y_recv, side_send, side_recv, small_send, small_recv,
+    mix_send, mix_recv, ready,
 ):
     me = lax.axis_index("ctx")
     ch = lax.axis_index("ch")
@@ -125,6 +131,8 @@
     to_chunks(lambda r: tile(f_ref, r), send_f)
 
     pl.semaphore_wait(barrier, N_CTX - 1 + N_CH - 1)
+    for o in range(1, N_CH):
+        pl.semaphore_signal(ready, inc=1, device_id=(me, lax.rem(ch + o, N_CH)), device_id_type=MESH)
 
     def chunk_copy(send, recv, s_sem, r_sem, peer):
         return pltpu.make_async_remote_copy(
@@ -132,14 +140,25 @@
             device_id=(peer, ch), device_id_type=MESH,
         )
 
+    def far_first(i):
+        j = i - 8
+        reach = 3 - j // 16
+        dz = jnp.where(j % 2 == 0, reach, 8 - reach)
+        inner = j % 16 // 2
+        dz, inner = jnp.where(i < 8, 4, dz), jnp.where(i < 8, i, inner)
+        dz, inner = jnp.where(i < 56, dz, 0), jnp.where(i < 56, inner, i - 55)
+        z, x, core = me // 8, me % 8 // 2, me % 2
+        z, x, core = (z + dz) % 8, (x + inner // 2) % 4, (core + inner) % 2
+        return z * 8 + x * 2 + core
+
     def scatter(send, recv, s_sem, r_sem):
         pltpu.make_async_copy(send.at[me], recv.at[me], r_sem).start()
 
-        def step(o, carry):
-            chunk_copy(send, recv, s_sem, r_sem, lax.rem(me + o, N_CTX)).start()
+        def step(i, carry):
+            chunk_copy(send, recv, s_sem, r_sem, far_first(i)).start()
             return carry
 
-        lax.fori_loop(1, N_CTX, step, 0)
+        lax.fori_loop(0, N_CTX - 1, step, 0)
 
     def whole(ref, s_sem, r_sem):
         return pltpu.make_async_remote_copy(
@@ -149,6 +168,29 @@
 
     scatter(send_s, recv_s, s_send, s_recv)
     scatter(send_f, recv_f, f_send, f_recv)
+
+    def to_peer(src, dst, s_sem, r_sem, o):
+        return pltpu.make_async_remote_copy(
+            src_ref=src, dst_ref=dst, send_sem=s_sem, recv_sem=r_sem,
+            device_id=(me, lax.rem(ch + o, N_CH)), device_id_type=MESH,
+        )
+
+    for copy in loads[3:]:
+        copy.wait()
+    for y in range(N_CH):
+        for i in range(PIECES):
+            src = slice(lane_tile(y, i) * 128, lane_tile(y, i) * 128 + 128)
+            dst = slice(i * 128, i * 128 + 128)
+            side_out[y, 0, :, dst] = q_ref[:, src]
+            side_out[y, 1, :, dst] = v_ref[:, src]
+    pl.semaphore_wait(ready, N_CH - 1)
+    for o in (2, 1, 3):
+        to_peer(skip_row, skip_all.at[ch], small_send.at[0], small_recv.at[0], o).start()
+        to_peer(w_ref, w_all.at[ch], small_send.at[1], small_recv.at[1], o).start()
+        to_peer(side_out.at[lax.rem(ch + o, N_CH)], side_in.at[ch], side_send, side_recv, o).start()
+    skip_all[ch] = skip_row[...]
+    w_all[ch] = w_ref[...]
+    side_in[ch] = side_out[ch]
 
     for copy in table_loads:
         copy.wait()
@@ -235,74 +277,79 @@
     per_group = A // GROUPS
     mine = me // GROUP
 
+    def group_at(i):
+        return jnp.where(i < 2, 2 - i, 9 - 3 * i)
+
     def inverse_step(i, carry):
-        g = lax.rem(mine + i, GROUPS)
+        g = lax.rem(mine + group_at(i), GROUPS)
         rows = pl.ds(pl.multiple_of(g * per_group, per_group), per_group)
         y = dot(ph[rows, :], y_hi[...]) + dot(plo[rows, :], y_hi[...]) + dot(ph[rows, :], y_lo[...])
-        half = ROWS // 2
-        y = jnp.concatenate(
-            [y[:, :128].reshape(GROUP, half, 128), y[:, 128:].reshape(GROUP, half, 128)], axis=1
-        )
-        send_y[pl.ds(g * GROUP, GROUP)] = y.astype(BF16)
+        for h in range(2):
+            part = y[:, h * 128 : h * 128 + 128].reshape(GROUP, 2, PIECES, 128).astype(BF16)
+            for p in range(2):
+                send_y[h * 2 + p, pl.ds(g * GROUP, GROUP)] = part[:, p]
 
         def step(o, carry):
-            peer = g * GROUP + lax.rem(me + o, GROUP)
-
-            @pl.when(peer != me)
+            peer = g * GROUP + lax.rem(me + o // N_CH, GROUP)
+            to = lax.rem(ch + o, N_CH)
+            own = jnp.logical_and(peer == me, to == ch)
+
+            @pl.when(jnp.logical_not(own))
             def _():
-                chunk_copy(send_y, recv_y, y_send, y_recv.at[mine], peer).start()
-
-            @pl.when(peer == me)
+                pltpu.make_async_remote_copy(
+                    src_ref=send_y.at[to, peer], dst_ref=recv_y.at[ch, me],
+                    send_sem=y_send, recv_sem=y_recv.at[ch],
+                    device_id=(peer, to), device_id_type=MESH,
+                ).start()
+
+            @pl.when(own)
             def _():
-                pltpu.make_async_copy(send_y.at[me], recv_y.at[me], y_recv.at[mine]).start()
+                pltpu.make_async_copy(send_y.at[to, peer], recv_y.at[ch, me], y_recv.at[ch]).start()
 
             return carry
 
-        return lax.fori_loop(0, GROUP, step, carry)
+        return lax.fori_loop(0, GROUP * N_CH, step, carry)
 
     lax.fori_loop(0, GROUPS, inverse_step, 0)
 
-    for copy in loads[3:]:
-        copy.wait()
+    three = pl.ds(0, N_CH - 1)
+    to_peer(skip_all.at[three], skip_all.at[three], small_send.at[0], small_recv.at[0], 1).wait_recv()
+    to_peer(w_all.at[three], w_all.at[three], small_send.at[1], small_recv.at[1], 1).wait_recv()
+    to_peer(side_in.at[three], side_in.at[three], side_send, side_recv, 1).wait_recv()
     eye = lax.broadcasted_iota(jnp.int32, (N_CTX, N_CTX), 0) == lax.broadcasted_iota(jnp.int32, (N_CTX, N_CTX), 1)
-    skip_ref[...] = jnp.where(eye, skip_row[...], 0.0)
-
-    def gate_copy(rows, o):
-        return pltpu.make_async_remote_copy(
-            src_ref=gathered.at[ch, rows], dst_ref=gathered.at[ch, rows],
-            send_sem=g_send, recv_sem=g_recv,
-            device_id=(me, lax.rem(ch + o, N_CH)), device_id_type=MESH,
-        )
-
-    for g in range(GROUPS):
-        rows = slice(g * GROUP, (g + 1) * GROUP)
-        whole(recv_y.at[rows], y_send, y_recv.at[g]).wait_recv()
-        conv32[...] = recv_y[rows].astype(F32).reshape(GROUP * ROWS, 128)
-        gain = jnp.sum(skip_ref[rows, :], axis=1, keepdims=True)
-        for r in range(ROWS):
-            lanes = slice(r * 128, (r + 1) * 128)
-            c = conv32[pl.ds(sub_row(r), GROUP, stride=ROWS), :]
-            gated = q_ref[rows, lanes].astype(F32) * (c + gain * v_ref[rows, lanes].astype(F32))
-            gathered[ch, rows, lanes] = gated.astype(BF16)
-        for o in (2, 1, 3):
-            gate_copy(pl.ds(g * GROUP, GROUP), o).start()
-
-    three = gathered.at[pl.ds(0, N_CH - 1)]
-    done = pltpu.make_async_remote_copy(
-        src_ref=three, dst_ref=three, send_sem=g_send, recv_sem=g_recv,
-        device_id=(me, lax.rem(ch + 1, N_CH)), device_id_type=MESH,
-    )
-    done.wait_recv()
-    for r in range(CHUNK // 512):
-        lanes = slice(r * 512, (r + 1) * 512)
-        mixed = dot(w_ref[...], gathered[:, :, lanes].reshape(N_CH * N_CTX, 512))
-        out_ref[:, lanes] = mixed.astype(BF16)
-
-    done.wait_send()
+    for y in range(N_CH):
+        gain = jnp.sum(jnp.where(eye, skip_all[y], 0.0), axis=1, keepdims=True)
+        gain_v[y] = gain * side_in[y, 1].astype(F32)
+
+    for y in range(N_CH):
+        whole(recv_y.at[y], y_send, y_recv.at[y]).wait_recv()
+        conv32[...] = recv_y[y].astype(F32).reshape(N_CTX * PIECES, 128)
+        for i in range(PIECES):
+            lanes = slice(i * 128, i * 128 + 128)
+            c = conv32[pl.ds(i, N_CTX, stride=PIECES), :]
+            value = side_in[y, 0, :, lanes].astype(F32) * (c + gain_v[y, :, lanes])
+            gated[y * N_CTX : (y + 1) * N_CTX, lanes] = value.astype(BF16)
+
+    mixed = dot(w_all[...].reshape(N_CH * N_CTX, N_CH * N_CTX), gated[...])
+    mix_out[...] = mixed.astype(BF16).reshape(N_CH, N_CTX, PIECES * 128)
+    for o in (2, 1, 3):
+        to_peer(mix_out.at[lax.rem(ch + o, N_CH)], mix_in.at[ch], mix_send, mix_recv, o).start()
+    mix_in[ch] = mix_out[ch]
+    to_peer(mix_in.at[three], mix_in.at[three], mix_send, mix_recv, 1).wait_recv()
+    for y in range(N_CH):
+        for i in range(PIECES):
+            at = lane_tile(y, i) * 128
+            out_ref[:, at : at + 128] = mix_in[y, :, i * 128 : i * 128 + 128]
+
+    to_peer(skip_all.at[three], skip_all.at[three], small_send.at[0], small_recv.at[0], 1).wait_send()
+    to_peer(w_all.at[three], w_all.at[three], small_send.at[1], small_recv.at[1], 1).wait_send()
+    to_peer(side_in.at[three], side_in.at[three], side_send, side_recv, 1).wait_send()
+    to_peer(mix_in.at[three], mix_in.at[three], mix_send, mix_recv, 1).wait_send()
     most = pl.ds(0, N_CTX - 1)
     whole(send_s.at[most], s_send, s_recv).wait_send()
     whole(send_f.at[most], f_send, f_recv).wait_send()
-    whole(send_y.at[most], y_send, y_recv.at[0]).wait_send()
+    whole(send_y.at[three], y_send, y_recv.at[0]).wait_send()
+    whole(send_y.at[0, most], y_send, y_recv.at[0]).wait_send()
 
 
 def on_device(value_in, key_gate, query_gate, filter_taps, skip_gain, out_weight):
@@ -311,6 +358,7 @@
     args += [jnp.asarray(c) for c in consts]
     vm = pltpu.VMEM
     copies = [vm((N_CTX, CHUNK), BF16)] * 3 + [vm((N_CTX, CHUNK), F32), vm((1, N_CTX), F32), vm((N_CTX, N_CH * N_CTX), BF16)]
+    copies += [vm((N_CH, 1, N_CTX), F32), vm((N_CH, N_CTX, N_CH * N_CTX), BF16)]
     copies += [vm(c.shape, c.dtype) for c in consts]
     copies += [vm((2 * A, A), BF16)] * 2 + [vm((A, 2 * A), BF16)] * 2 + [vm((2 * B, 2 * B), BF16)] * 4 + [vm((A, B), F32)] * 2
     chunk = vm((N_CTX, ROWS, 128), BF16)
@@ -322,16 +370,23 @@
         out_specs=pl.BlockSpec(memory_space=pltpu.VMEM),
         scratch_shapes=copies
         + [vm((N_CTX * ROWS, 128), F32)]
-        + [chunk] * 6
+        + [chunk] * 2
+        + [vm((N_CH, N_CTX, PIECES, 128), BF16)]
+        + [chunk] * 2
+        + [vm((N_CH, N_CTX, PIECES, 128), BF16)]
+        + [vm((N_CH, 2, N_CTX, CHUNK // N_CH), BF16)] * 2
         + [
-            vm((N_CTX, N_CTX), F32),
+            vm((N_CH, N_CTX, CHUNK // N_CH), F32),
             vm((A, B), BF16),
             vm((A, 2 * B), F32),
             vm((2 * A, B), BF16),
             vm((2 * A, B), BF16),
-            vm((GROUP * ROWS, 128), F32),
-            vm((N_CH, N_CTX, CHUNK), BF16),
-            dma((6,)), dma((8,)), dma, dma, dma, dma, dma, dma((GROUPS,)), dma, dma,
+            vm((N_CTX * PIECES, 128), F32),
+            vm((N_CH * N_CTX, CHUNK // N_CH), BF16),
+            vm((N_CH, N_CTX, CHUNK // N_CH), BF16),
+            vm((N_CH, N_CTX, CHUNK // N_CH), BF16),
+            dma((6,)), dma((8,)), dma, dma, dma, dma, dma, dma((N_CH,)), dma, dma, dma((2,)), dma((2,)),
+            dma, dma, pltpu.SemaphoreType.REGULAR,
         ],
         compiler_params=pltpu.CompilerParams(
             collective_id=0, has_side_effects=True, vmem_limit_bytes=56 * 1024 * 1024

time: 54.8 us -> 50.7 us (0.925)
  Pallas kernels: 53 us -> 48.9 us
    pallas_call x1, Pallas kernels: 53 us -> 48.9 us  [on_device(): pl.pallas_call(kernel, out_shape=jax.ShapeDtypeStruct((N_CTX, CHUNK), BF1...]
where the time goes in v3:
time: 50.7 us; the launch traced here: 50.6 us
  Pallas kernels  48.9 us (96%)
  local copies, waits for them, and re-layouts  1.67 us (3%)
    pallas_call x1, Pallas kernels, on_device(): pl.pallas_call(kernel, out_shape=jax.ShapeDtypeStruct((N_CTX, CHUNK), BF1...  48.9 us
    unnamed x1, local copies, waits for them, and re-layouts  1.67 us

profile of v3, /device:TPU:1, one launch (start us, length us, event | category | flops | bytes accessed | tf_op | source)
XLA Modules:
  0.0 50.6 jit_solution(16993788039389107100)
XLA Ops:
  0.0 48.9 %hyena.1 = bf16[64,2048]{1,0:T(8,128)(2,1)} custom-call(bf16[64,2048]{1,0:T(8,128)(2,1)} %v_hbm.1, bf16[64,2048]{1,0:T(8,128)(2,1)} %k_hbm.1, bf16[64,2048]{1,0:T(8,128)(2,1)} %q_hbm.1, f32[64,2048]{1,0:T(8,128)} %f_hbm.1, f32[1,64]{1,0:T(1,128)} %bitcast.3, bf16[64,256]{1,0:T(8,128)(2,1)} %bitcast.2, f32[2,32,512]{2,1,0:T(8,128)} %constant.16.clone.fa_hbm, ...), custom_call_target="tpu_custom_call" | custom-call | tf_op jit(solution)/shard_map/hyena/pallas_call | solution.py:366
  48.9 1.7 %copy.16 = bf16[64,2048]{1,0:T(8,128)(2,1)} copy(bf16[64,2048]{1,0:T(8,128)(2,1)} %hyena.1) | data formatting | bytes 524288

commit v4 on v3

--- a/solution.py
+++ b/solution.py
@@ -17,12 +17,10 @@
 CHUNK = 2048
 ROWS = 16
 T = N_CTX * CHUNK
-A = 512
-B = 256
-GROUP = 16
-GROUPS = N_CTX // GROUP
+A = 256
+B = 512
 PIECES = ROWS // N_CH
-TILE = 256
+TILE = 32
 
 
 def turns(rows, columns):
@@ -33,12 +31,19 @@
 @functools.cache
 def tables():
     coarse, fine = 16 * np.arange(A // 16), np.arange(16)
-    column = np.arange(A)
+    freq, column = np.arange(A) + 0.25, np.arange(B)
+    inner = (4 * np.arange(128)[None, :] + np.arange(4)[:, None]).reshape(-1) / B
+    lanes = np.tile(np.arange(128), 4)
+    back = turns(fine, 4 * lanes / B)
+    shift = np.repeat(np.arange(4), 128) * lanes / B
+    cs, sn = np.cos(2 * np.pi * shift), np.sin(2 * np.pi * shift)
+    back = np.stack([back[0] * cs - back[1] * sn, back[1] * cs + back[0] * sn]).astype(np.float32)
     return (
-        turns(coarse, column / A), turns(fine + 0.25, column / A),
-        turns(coarse, (column + 0.25) / A), turns(fine, (column + 0.25) / A),
-        turns(coarse[: B // 16], np.arange(B) / B), turns(fine, np.arange(B) / B),
-        turns(coarse, np.arange(B) / T), turns(fine + 0.25, np.arange(B) / T),
+        turns(coarse, np.arange(A) / A), turns(fine + 0.25, np.arange(A) / A),
+        turns(coarse, freq / A), turns(fine, freq / A),
+        turns(coarse[:8], inner), turns(fine, inner),
+        turns(coarse[:8], 4 * lanes / B), back,
+        turns(coarse, column / T), turns(fine + 0.25, column / T),
     )
 
 
@@ -51,36 +56,42 @@
     return high, (x - high.astype(F32)).astype(BF16)
 
 
-def times_right(x, table_hi, table_lo):
-    high, low = parts_of(x)
-    return dot(high, table_hi[...]) + dot(high, table_lo[...]) + dot(low, table_hi[...])
-
-
-def sub_row(r):
-    return (r % 2) * (ROWS // 2) + r // 2
-
-
 def lane_tile(y, i):
-    return 8 * (y % 2) + 2 * i + y // 2
-
-
-def chunks_to_matrix(recv):
-    x = recv[...].astype(F32)
-    half = ROWS // 2
-    left = x[:, :half, :].reshape(A, 128)
-    right = x[:, half:, :].reshape(A, 128)
-    return jnp.concatenate([left, right], axis=1).astype(BF16)
+    return 4 * i + y
+
+
+def mul(a, b):
+    return a[0] * b[0] - a[1] * b[1], a[0] * b[1] + a[1] * b[0]
+
+
+def mul_conj(a, b):
+    return a[0] * b[0] + a[1] * b[1], a[1] * b[0] - a[0] * b[1]
+
+
+def add(a, b):
+    return a[0] + b[0], a[1] + b[1]
+
+
+def sub(a, b):
+    return a[0] - b[0], a[1] - b[1]
+
+
+def four_point(x, sign):
+    even, odd = add(x[0], x[2]), add(x[1], x[3])
+    even_d, odd_d = sub(x[0], x[2]), sub(x[1], x[3])
+    turned = (-sign * odd_d[1], sign * odd_d[0])
+    return add(even, odd), add(even_d, turned), sub(even, odd), sub(even_d, turned)
 
 
 def kernel(
     v_hbm, k_hbm, q_hbm, f_hbm, skip_hbm, w_hbm,
-    fa_hbm, fb_hbm, ga_hbm, gb_hbm, ia_hbm, ib_hbm, ta_hbm, tb_hbm,
+    fa_hbm, fb_hbm, ga_hbm, gb_hbm, ia_hbm, ib_hbm, ja_hbm, jb_hbm, ta_hbm, tb_hbm,
     out_ref,
     v_ref, k_ref, q_ref, f_ref, skip_row, w_ref, skip_all, w_all,
-    fa, fb, ga, gb, ia, ib, ta, tb,
+    fa, fb, ga, gb, ia, ib, ja, jb, ta, tb,
     oh, ol, ph, plo, ah, al, bh, bl, tc, ts,
     stage, send_s, send_f, send_y, recv_s, recv_f, recv_y,
-    side_out, side_in, gain_v, x_ref, spec, y_hi, y_lo, conv32, gated, mix_out, mix_in,
+    side_out, side_in, gain_v, x_ref, z_ref, s_hi, s_lo, spec, f_spec, y_hi, y_lo, conv32, gated, mix_out, mix_in,
     in_sem, table_sem, s_send, s_recv, f_send, f_recv, y_send, y_recv, side_send, side_recv, small_send, small_recv,
     mix_send, mix_recv, ready,
 ):
@@ -97,8 +108,8 @@
         pltpu.make_async_copy(src, dst, table_sem.at[i])
         for i, (src, dst) in enumerate(
             zip(
-                (fa_hbm, fb_hbm, ga_hbm, gb_hbm, ia_hbm, ib_hbm, ta_hbm, tb_hbm),
-                (fa, fb, ga, gb, ia, ib, ta, tb),
+                (fa_hbm, fb_hbm, ga_hbm, gb_hbm, ia_hbm, ib_hbm, ja_hbm, jb_hbm, ta_hbm, tb_hbm),
+                (fa, fb, ga, gb, ia, ib, ja, jb, ta, tb),
             )
         )
     ]
@@ -107,18 +118,20 @@
 
     barrier = pltpu.get_barrier_semaphore()
 
+    def wrap(value, size):
+        return jnp.where(value >= size, value - size, value)
+
     def greet(o, carry):
-        peer = lax.rem(me + o, N_CTX)
-        pl.semaphore_signal(barrier, inc=1, device_id=(peer, ch), device_id_type=MESH)
+        pl.semaphore_signal(barrier, inc=1, device_id=(wrap(me + o, N_CTX), ch), device_id_type=MESH)
         return carry
 
-    lax.fori_loop(1, N_CTX, greet, 0)
+    lax.fori_loop(1, N_CTX, greet, 0, unroll=3)
     for o in range(1, N_CH):
         pl.semaphore_signal(barrier, inc=1, device_id=(me, lax.rem(ch + o, N_CH)), device_id_type=MESH)
 
     def to_chunks(value, send):
         for r in range(ROWS):
-            stage[pl.ds(sub_row(r), N_CTX, stride=ROWS), :] = value(r)
+            stage[pl.ds(r, N_CTX, stride=ROWS), :] = value(r)
         send[...] = stage[...].astype(BF16).reshape(N_CTX, ROWS, 128)
 
     def tile(ref, r):
@@ -140,25 +153,26 @@
             device_id=(peer, ch), device_id_type=MESH,
         )
 
-    def far_first(i):
-        j = i - 8
-        reach = 3 - j // 16
-        dz = jnp.where(j % 2 == 0, reach, 8 - reach)
-        inner = j % 16 // 2
-        dz, inner = jnp.where(i < 8, 4, dz), jnp.where(i < 8, i, inner)
-        dz, inner = jnp.where(i < 56, dz, 0), jnp.where(i < 56, inner, i - 55)
-        z, x, core = me // 8, me % 8 // 2, me % 2
-        z, x, core = (z + dz) % 8, (x + inner // 2) % 4, (core + inner) % 2
-        return z * 8 + x * 2 + core
+    z, lane = me // 8, me % 8
 
     def scatter(send, recv, s_sem, r_sem):
+        for offsets in ((4,), (3, 5), (2, 6), (1, 7)):
+            bases = [wrap(z + dz, 8) * 8 for dz in offsets]
+
+            def step(i, carry, bases=bases):
+                to = wrap(lane + i, 8)
+                for base in bases:
+                    chunk_copy(send, recv, s_sem, r_sem, base + to).start()
+                return carry
+
+            lax.fori_loop(0, 8, step, 0, unroll=2)
+
+        def near(i, carry):
+            chunk_copy(send, recv, s_sem, r_sem, z * 8 + wrap(lane + i, 8)).start()
+            return carry
+
+        lax.fori_loop(1, 8, near, 0)
         pltpu.make_async_copy(send.at[me], recv.at[me], r_sem).start()
-
-        def step(i, carry):
-            chunk_copy(send, recv, s_sem, r_sem, far_first(i)).start()
-            return carry
-
-        lax.fori_loop(0, N_CTX - 1, step, 0)
 
     def whole(ref, s_sem, r_sem):
         return pltpu.make_async_remote_copy(
@@ -209,108 +223,122 @@
         c, s = block(fa, fb, i)
         put(oh, ol, (up,), c)
         put(oh, ol, (down,), -s)
+        c, s = block(ga, gb, i)
+        put(ph, plo, (up, slice(0, A)), c * (1.0 / T))
+        put(ph, plo, (up, slice(A, 2 * A)), s * (-1.0 / T))
         c, s = block(ta, tb, i)
         tc[up, :], ts[up, :] = c, -s
         return carry
 
     def make_inner(i, carry):
         up = pl.ds(pl.multiple_of(i * 16, 16), 16)
-        down = pl.ds(pl.multiple_of(B + i * 16, 16), 16)
-        left, right = slice(0, B), slice(B, 2 * B)
-        c, s = block(ia, ib, i)
-        for high, low, sign in ((ah, al, 1.0), (bh, bl, -1.0)):
-            put(high, low, (up, left), c)
-            put(high, low, (down, right), c)
-            put(high, low, (up, right), -sign * s)
-            put(high, low, (down, left), sign * s)
+        down = pl.ds(pl.multiple_of(128 + i * 16, 16), 16)
+        left, right = slice(0, 128), slice(128, 256)
+        for high, low, coarse, fine, sign in ((ah, al, ia, ib, 1.0), (bh, bl, ja, jb, -1.0)):
+            c, s = block(coarse, fine, i)
+            for k in range(4):
+                ck, sk = c[:, k * 128 : k * 128 + 128], s[:, k * 128 : k * 128 + 128]
+                put(high, low, (k, up, left), ck)
+                put(high, low, (k, down, right), ck)
+                put(high, low, (k, up, right), -sign * sk)
+                put(high, low, (k, down, left), sign * sk)
         return carry
 
-    def make_last(i, carry):
-        up = pl.ds(pl.multiple_of(i * 16, 16), 16)
-        c, s = block(ga, gb, i)
-        put(ph, plo, (up, slice(0, A)), c * (1.0 / T))
-        put(ph, plo, (up, slice(A, 2 * A)), s * (-1.0 / T))
-        return carry
-
     lax.fori_loop(0, A // 16, make_outer, 0)
-    lax.fori_loop(0, B // 16, make_inner, 0)
-    lax.fori_loop(0, A // 16, make_last, 0)
-
-    def forward(row):
-        x = x_ref[...]
-        up, down = pl.ds(row, TILE), pl.ds(A + row, TILE)
-        re = dot(oh[up, :], x) + dot(ol[up, :], x)
-        im = dot(oh[down, :], x) + dot(ol[down, :], x)
-        c, s = tc[up, :], ts[up, :]
-        return times_right(jnp.concatenate([re * c - im * s, re * s + im * c], axis=1), ah, al)
+    lax.fori_loop(0, 8, make_inner, 0)
+
+    def load_matrix(recv):
+        stage[...] = recv[...].astype(F32).reshape(N_CTX * ROWS, 128)
+        for r in range(4):
+            x_ref[:, r * 128 : r * 128 + 128] = stage[pl.ds(r, A, stride=4), :].astype(BF16)
+
+    def pair(ref, rows, k, imag):
+        return ref[rows, k * 128 : k * 128 + 128], ref[imag, k * 128 : k * 128 + 128]
+
+    def put_pair(k, rows, value):
+        for part, at in ((value[0], k * 256), (value[1], k * 256 + 128)):
+            s_hi[rows, at : at + 128], s_lo[rows, at : at + 128] = parts_of(part)
+
+    def inner(high, low, k):
+        at = slice(k * 256, k * 256 + 256)
+        return dot(s_hi[:, at], high[k]) + dot(s_hi[:, at], low[k]) + dot(s_lo[:, at], high[k])
+
+    def forward(recv, out):
+        load_matrix(recv)
+        z_ref[...] = dot(oh[...], x_ref[...]) + dot(ol[...], x_ref[...])
+        for row in range(0, A, TILE):
+            rows, imag = slice(row, row + TILE), slice(A + row, A + row + TILE)
+            turned = []
+            for r in range(4):
+                at = slice(r * 128, r * 128 + 128)
+                turned.append(mul(pair(z_ref, rows, r, imag), (tc[rows, at], ts[rows, at])))
+            for k, value in enumerate(four_point(turned, -1.0)):
+                put_pair(k, rows, value)
+        for k in range(4):
+            out[:, k * 256 : k * 256 + 256] = inner(ah, al, k)
 
     whole(recv_s, s_send, s_recv).wait_recv()
-    x_ref[...] = chunks_to_matrix(recv_s)
-
-    def signal_step(i, carry):
-        row = pl.multiple_of(i * TILE, TILE)
-        spec[pl.ds(row, TILE), :] = forward(row)
-        return carry
-
-    lax.fori_loop(0, A // TILE, signal_step, 0)
+    forward(recv_s, spec)
 
     whole(recv_f, f_send, f_recv).wait_recv()
-    x_ref[...] = chunks_to_matrix(recv_f)
-
-    def taps_step(i, carry):
-        row = pl.multiple_of(i * TILE, TILE)
-        up, down = pl.ds(row, TILE), pl.ds(A + row, TILE)
-        taps = forward(row)
-        fr, fi = taps[:, :B], taps[:, B:]
-        sr, si = spec[up, :B], spec[up, B:]
-        product = jnp.concatenate([sr * fr - si * fi, sr * fi + si * fr], axis=1)
-        y = times_right(product, bh, bl)
-        re, im = y[:, :B], y[:, B:]
-        c, s = tc[up, :], ts[up, :]
-        re, im = re * c + im * s, im * c - re * s
-        y_hi[up, :], y_lo[up, :] = parts_of(re)
-        y_hi[down, :], y_lo[down, :] = parts_of(im)
-        return carry
-
-    lax.fori_loop(0, A // TILE, taps_step, 0)
-
-    per_group = A // GROUPS
-    mine = me // GROUP
-
-    def group_at(i):
-        return jnp.where(i < 2, 2 - i, 9 - 3 * i)
-
-    def inverse_step(i, carry):
-        g = lax.rem(mine + group_at(i), GROUPS)
-        rows = pl.ds(pl.multiple_of(g * per_group, per_group), per_group)
-        y = dot(ph[rows, :], y_hi[...]) + dot(plo[rows, :], y_hi[...]) + dot(ph[rows, :], y_lo[...])
-        for h in range(2):
-            part = y[:, h * 128 : h * 128 + 128].reshape(GROUP, 2, PIECES, 128).astype(BF16)
-            for p in range(2):
-                send_y[h * 2 + p, pl.ds(g * GROUP, GROUP)] = part[:, p]
-
-        def step(o, carry):
-            peer = g * GROUP + lax.rem(me + o // N_CH, GROUP)
-            to = lax.rem(ch + o, N_CH)
-            own = jnp.logical_and(peer == me, to == ch)
-
-            @pl.when(jnp.logical_not(own))
+    forward(recv_f, f_spec)
+    for k in range(4):
+        at, half = slice(k * 256, k * 256 + 128), slice(k * 256 + 128, k * 256 + 256)
+        for row in range(0, A, TILE):
+            rows = slice(row, row + TILE)
+            put_pair(k, rows, mul((spec[rows, at], spec[rows, half]), (f_spec[rows, at], f_spec[rows, half])))
+        f_spec[:, k * 256 : k * 256 + 256] = inner(bh, bl, k)
+    for row in range(0, A, TILE):
+        rows, imag = slice(row, row + TILE), slice(A + row, A + row + TILE)
+        back = [
+            (f_spec[rows, k * 256 : k * 256 + 128], f_spec[rows, k * 256 + 128 : k * 256 + 256]) for k in range(4)
+        ]
+        for r, value in enumerate(four_point(back, 1.0)):
+            at = slice(r * 128, r * 128 + 128)
+            re, im = mul_conj(value, (tc[rows, at], ts[rows, at]))
+            y_hi[rows, at], y_lo[rows, at] = parts_of(re)
+            y_hi[imag, at], y_lo[imag, at] = parts_of(im)
+
+    sides = [wrap(ch + k, N_CH) for k in range(N_CH)]
+
+    def piece_copy(peer, to):
+        return pltpu.make_async_remote_copy(
+            src_ref=send_y.at[to, peer], dst_ref=recv_y.at[ch, me], send_sem=y_send, recv_sem=y_recv.at[ch],
+            device_id=(peer, to), device_id_type=MESH,
+        )
+
+    def send_pieces(quarters):
+        for offsets in ((4,), (3, 5), (2, 6), (1, 7)):
+            bases = [wrap(z + dz, 8) * 8 for dz in offsets]
+
+            def step(i, carry, bases=bases):
+                to = wrap(lane + i, 8)
+                for y in quarters:
+                    for base in bases:
+                        piece_copy(base + to, y).start()
+                return carry
+
+            lax.fori_loop(0, 8, step, 0, unroll=4 // len(offsets))
+
+        def near(i, carry):
+            for y in quarters:
+                piece_copy(z * 8 + wrap(lane + i, 8), y).start()
+            return carry
+
+        lax.fori_loop(1, 8, near, 0)
+        for y in quarters:
+
+            @pl.when(y != ch)
             def _():
-                pltpu.make_async_remote_copy(
-                    src_ref=send_y.at[to, peer], dst_ref=recv_y.at[ch, me],
-                    send_sem=y_send, recv_sem=y_recv.at[ch],
-                    device_id=(peer, to), device_id_type=MESH,
-                ).start()
-
-            @pl.when(own)
-            def _():
-                pltpu.make_async_copy(send_y.at[to, peer], recv_y.at[ch, me], y_recv.at[ch]).start()
-
-            return carry
-
-        return lax.fori_loop(0, GROUP * N_CH, step, carry)
-
-    lax.fori_loop(0, GROUPS, inverse_step, 0)
+                piece_copy(me, y).start()
+
+    for first in (0, 2):
+        at = slice(first * 128, first * 128 + 256)
+        y = dot(ph[...], y_hi[:, at]) + dot(plo[...], y_hi[:, at]) + dot(ph[...], y_lo[:, at])
+        for r in range(2):
+            send_y[first + r] = y[:, r * 128 : r * 128 + 128].reshape(N_CTX, PIECES, 128).astype(BF16)
+        send_pieces((first, first + 1))
+    pltpu.make_async_copy(send_y.at[ch, me], recv_y.at[ch, me], y_recv.at[ch]).start()
 
     three = pl.ds(0, N_CH - 1)
     to_peer(skip_all.at[three], skip_all.at[three], small_send.at[0], small_recv.at[0], 1).wait_recv()
@@ -360,7 +388,7 @@
     copies = [vm((N_CTX, CHUNK), BF16)] * 3 + [vm((N_CTX, CHUNK), F32), vm((1, N_CTX), F32), vm((N_CTX, N_CH * N_CTX), BF16)]
     copies += [vm((N_CH, 1, N_CTX), F32), vm((N_CH, N_CTX, N_CH * N_CTX), BF16)]
     copies += [vm(c.shape, c.dtype) for c in consts]
-    copies += [vm((2 * A, A), BF16)] * 2 + [vm((A, 2 * A), BF16)] * 2 + [vm((2 * B, 2 * B), BF16)] * 4 + [vm((A, B), F32)] * 2
+    copies += [vm((2 * A, A), BF16)] * 2 + [vm((A, 2 * A), BF16)] * 2 + [vm((4, 256, 256), BF16)] * 4 + [vm((A, B), F32)] * 2
     chunk = vm((N_CTX, ROWS, 128), BF16)
     dma = pltpu.SemaphoreType.DMA
     return pl.pallas_call(
@@ -378,6 +406,10 @@
         + [
             vm((N_CH, N_CTX, CHUNK // N_CH), F32),
             vm((A, B), BF16),
+            vm((2 * A, B), F32),
+            vm((A, 2 * B), BF16),
+            vm((A, 2 * B), BF16),
+            vm((A, 2 * B), F32),
             vm((A, 2 * B), F32),
             vm((2 * A, B), BF16),
             vm((2 * A, B), BF16),
@@ -385,7 +417,7 @@
             vm((N_CH * N_CTX, CHUNK // N_CH), BF16),
             vm((N_CH, N_CTX, CHUNK // N_CH), BF16),
             vm((N_CH, N_CTX, CHUNK // N_CH), BF16),
-            dma((6,)), dma((8,)), dma, dma, dma, dma, dma, dma((N_CH,)), dma, dma, dma((2,)), dma((2,)),
+            dma((6,)), dma((10,)), dma, dma, dma, dma, dma, dma((N_CH,)), dma, dma, dma((2,)), dma((2,)),
             dma, dma, pltpu.SemaphoreType.REGULAR,
         ],
         compiler_params=pltpu.CompilerParams(

time: 50.7 us -> 48.3 us (0.953)
  Pallas kernels: 48.9 us -> 46.5 us
    pallas_call x1, Pallas kernels: 48.9 us -> 46.5 us  [on_device(): pl.pallas_call(kernel, out_shape=jax.ShapeDtypeStruct((N_CTX, CHUNK), BF1...]
where the time goes in v4:
time: 48.3 us; the launch traced here: 48.2 us
  Pallas kernels  46.5 us (96%)
  local copies, waits for them, and re-layouts  1.67 us (3%)
    pallas_call x1, Pallas kernels, on_device(): pl.pallas_call(kernel, out_shape=jax.ShapeDtypeStruct((N_CTX, CHUNK), BF1...  46.5 us
    unnamed x1, local copies, waits for them, and re-layouts  1.67 us

profile of v4, /device:TPU:1, one launch (start us, length us, event | category | flops | bytes accessed | tf_op | source)
XLA Modules:
  0.0 48.2 jit_solution(16169095111148079247)
XLA Ops:
  0.0 46.5 %hyena.1 = bf16[64,2048]{1,0:T(8,128)(2,1)} custom-call(bf16[64,2048]{1,0:T(8,128)(2,1)} %v_hbm.1, bf16[64,2048]{1,0:T(8,128)(2,1)} %k_hbm.1, bf16[64,2048]{1,0:T(8,128)(2,1)} %q_hbm.1, f32[64,2048]{1,0:T(8,128)} %f_hbm.1, f32[1,64]{1,0:T(1,128)} %bitcast.3, bf16[64,256]{1,0:T(8,128)(2,1)} %bitcast.2, f32[2,16,256]{2,1,0:T(8,128)} %constant.20.clone.fa_hbm, ...), custom_call_target="tpu_custom_call" | custom-call | tf_op jit(solution)/shard_map/hyena/pallas_call | solution.py:394
  46.5 1.7 %copy.18 = bf16[64,2048]{1,0:T(8,128)(2,1)} copy(bf16[64,2048]{1,0:T(8,128)(2,1)} %hyena.1) | data formatting | bytes 524288

commit v5 on v4

--- a/solution.py
+++ b/solution.py
@@ -98,6 +98,29 @@
     me = lax.axis_index("ctx")
     ch = lax.axis_index("ch")
 
+    barrier = pltpu.get_barrier_semaphore()
+
+    def wrap(value, size):
+        return jnp.where(value >= size, value - size, value)
+
+    z, lane = me // 8, me % 8
+
+    def greet(bases):
+        def step(i, carry):
+            to = wrap(lane + i, 8)
+            for base in bases:
+                pl.semaphore_signal(barrier, inc=1, device_id=(base + to, ch), device_id_type=MESH)
+            return carry
+
+        return step
+
+    away = [[wrap(z + dz, 8) * 8 for dz in offsets] for offsets in ((4,), (3, 5), (2, 6), (1, 7))]
+    for bases in away:
+        lax.fori_loop(0, 8, greet(bases), 0, unroll=4)
+    for o in range(1, N_CH):
+        pl.semaphore_signal(barrier, inc=1, device_id=(me, wrap(ch + o, N_CH)), device_id_type=MESH)
+    lax.fori_loop(1, 8, greet([z * 8]), 0)
+
     loads = [
         pltpu.make_async_copy(src, dst, in_sem.at[i])
         for i, (src, dst) in enumerate(
@@ -116,19 +139,6 @@
     for copy in loads + table_loads:
         copy.start()
 
-    barrier = pltpu.get_barrier_semaphore()
-
-    def wrap(value, size):
-        return jnp.where(value >= size, value - size, value)
-
-    def greet(o, carry):
-        pl.semaphore_signal(barrier, inc=1, device_id=(wrap(me + o, N_CTX), ch), device_id_type=MESH)
-        return carry
-
-    lax.fori_loop(1, N_CTX, greet, 0, unroll=3)
-    for o in range(1, N_CH):
-        pl.semaphore_signal(barrier, inc=1, device_id=(me, lax.rem(ch + o, N_CH)), device_id_type=MESH)
-
     def to_chunks(value, send):
         for r in range(ROWS):
             stage[pl.ds(r, N_CTX, stride=ROWS), :] = value(r)
@@ -144,20 +154,14 @@
     to_chunks(lambda r: tile(f_ref, r), send_f)
 
     pl.semaphore_wait(barrier, N_CTX - 1 + N_CH - 1)
-    for o in range(1, N_CH):
-        pl.semaphore_signal(ready, inc=1, device_id=(me, lax.rem(ch + o, N_CH)), device_id_type=MESH)
-
     def chunk_copy(send, recv, s_sem, r_sem, peer):
         return pltpu.make_async_remote_copy(
             src_ref=send.at[peer], dst_ref=recv.at[me], send_sem=s_sem, recv_sem=r_sem,
             device_id=(peer, ch), device_id_type=MESH,
         )
 
-    z, lane = me // 8, me % 8
-
     def scatter(send, recv, s_sem, r_sem):
-        for offsets in ((4,), (3, 5), (2, 6), (1, 7)):
-            bases = [wrap(z + dz, 8) * 8 for dz in offsets]
+        for bases in away:
 
             def step(i, carry, bases=bases):
                 to = wrap(lane + i, 8)
@@ -182,6 +186,8 @@
 
     scatter(send_s, recv_s, s_send, s_recv)
     scatter(send_f, recv_f, f_send, f_recv)
+    for o in range(1, N_CH):
+        pl.semaphore_signal(ready, inc=1, device_id=(me, lax.rem(ch + o, N_CH)), device_id_type=MESH)
 
     def to_peer(src, dst, s_sem, r_sem, o):
         return pltpu.make_async_remote_copy(
@@ -307,37 +313,26 @@
             device_id=(peer, to), device_id_type=MESH,
         )
 
-    def send_pieces(quarters):
-        for offsets in ((4,), (3, 5), (2, 6), (1, 7)):
-            bases = [wrap(z + dz, 8) * 8 for dz in offsets]
-
-            def step(i, carry, bases=bases):
-                to = wrap(lane + i, 8)
-                for y in quarters:
-                    for base in bases:
-                        piece_copy(base + to, y).start()
-                return carry
-
-            lax.fori_loop(0, 8, step, 0, unroll=4 // len(offsets))
-
-        def near(i, carry):
-            for y in quarters:
-                piece_copy(z * 8 + wrap(lane + i, 8), y).start()
-            return carry
-
-        lax.fori_loop(1, 8, near, 0)
-        for y in quarters:
-
-            @pl.when(y != ch)
-            def _():
-                piece_copy(me, y).start()
-
     for first in (0, 2):
         at = slice(first * 128, first * 128 + 256)
         y = dot(ph[...], y_hi[:, at]) + dot(plo[...], y_hi[:, at]) + dot(ph[...], y_lo[:, at])
         for r in range(2):
             send_y[first + r] = y[:, r * 128 : r * 128 + 128].reshape(N_CTX, PIECES, 128).astype(BF16)
-        send_pieces((first, first + 1))
+
+    for to_z in (0, 1, 2, 3, 4, 7, 5, 6):
+
+        def step(i, carry, base=to_z * 8):
+            peer = base + wrap(lane + i, 8)
+            for k in (2, 1, 3):
+                piece_copy(peer, sides[k]).start()
+
+            @pl.when(peer != me)
+            def _():
+                piece_copy(peer, ch).start()
+
+            return carry
+
+        lax.fori_loop(0, 8, step, 0, unroll=2)
     pltpu.make_async_copy(send_y.at[ch, me], recv_y.at[ch, me], y_recv.at[ch]).start()
 
     three = pl.ds(0, N_CH - 1)

time: 48.3 us -> 46.1 us (0.954)
  Pallas kernels: 46.5 us -> 44.1 us
    pallas_call x1, Pallas kernels: 46.5 us -> 44.1 us  [on_device(): pl.pallas_call(kernel, out_shape=jax.ShapeDtypeStruct((N_CTX, CHUNK), BF1...]
where the time goes in v5:
time: 46.1 us; the launch traced here: 45.8 us
  Pallas kernels  44.1 us (96%)
  local copies, waits for them, and re-layouts  1.67 us (4%)
    pallas_call x1, Pallas kernels, on_device(): pl.pallas_call(kernel, out_shape=jax.ShapeDtypeStruct((N_CTX, CHUNK), BF1...  44.1 us
    unnamed x1, local copies, waits for them, and re-layouts  1.67 us

profile of v5, /device:TPU:1, one launch (start us, length us, event | category | flops | bytes accessed | tf_op | source)
XLA Modules:
  0.0 45.8 jit_solution(12212033094611492076)
XLA Ops:
  0.0 44.1 %hyena.1 = bf16[64,2048]{1,0:T(8,128)(2,1)} custom-call(bf16[64,2048]{1,0:T(8,128)(2,1)} %v_hbm.1, bf16[64,2048]{1,0:T(8,128)(2,1)} %k_hbm.1, bf16[64,2048]{1,0:T(8,128)(2,1)} %q_hbm.1, f32[64,2048]{1,0:T(8,128)} %f_hbm.1, f32[1,64]{1,0:T(1,128)} %bitcast.3, bf16[64,256]{1,0:T(8,128)(2,1)} %bitcast.2, f32[2,16,256]{2,1,0:T(8,128)} %constant.20.clone.fa_hbm, ...), custom_call_target="tpu_custom_call" | custom-call | tf_op jit(solution)/shard_map/hyena/pallas_call | solution.py:389
  44.1 1.7 %copy.18 = bf16[64,2048]{1,0:T(8,128)(2,1)} copy(bf16[64,2048]{1,0:T(8,128)(2,1)} %hyena.1) | data formatting | bytes 524288

commit v6 on v5

--- a/solution.py
+++ b/solution.py
@@ -160,23 +160,27 @@
             device_id=(peer, ch), device_id_type=MESH,
         )
 
-    def scatter(send, recv, s_sem, r_sem):
+    def scatter(send, recv, s_sem, r_sem, core):
         for bases in away:
 
             def step(i, carry, bases=bases):
-                to = wrap(lane + i, 8)
+                to = wrap(lane // 2 + i, 4) * 2 + core
                 for base in bases:
                     chunk_copy(send, recv, s_sem, r_sem, base + to).start()
                 return carry
 
-            lax.fori_loop(0, 8, step, 0, unroll=2)
+            lax.fori_loop(0, 4, step, 0, unroll=2)
 
         def near(i, carry):
-            chunk_copy(send, recv, s_sem, r_sem, z * 8 + wrap(lane + i, 8)).start()
+            peer = z * 8 + wrap(lane // 2 + i, 4) * 2 + core
+
+            @pl.when(peer != me)
+            def _():
+                chunk_copy(send, recv, s_sem, r_sem, peer).start()
+
             return carry
 
-        lax.fori_loop(1, 8, near, 0)
-        pltpu.make_async_copy(send.at[me], recv.at[me], r_sem).start()
+        lax.fori_loop(0, 4, near, 0)
 
     def whole(ref, s_sem, r_sem):
         return pltpu.make_async_remote_copy(
@@ -184,8 +188,14 @@
             device_id=(lax.rem(me + 1, N_CTX), ch), device_id_type=MESH,
         )
 
-    scatter(send_s, recv_s, s_send, s_recv)
-    scatter(send_f, recv_f, f_send, f_recv)
+    def scatter_both(core, carry):
+        scatter(send_s, recv_s, s_send, s_recv, core)
+        scatter(send_f, recv_f, f_send, f_recv, core)
+        return carry
+
+    lax.fori_loop(0, 2, scatter_both, 0)
+    pltpu.make_async_copy(send_s.at[me], recv_s.at[me], s_recv).start()
+    pltpu.make_async_copy(send_f.at[me], recv_f.at[me], f_recv).start()
     for o in range(1, N_CH):
         pl.semaphore_signal(ready, inc=1, device_id=(me, lax.rem(ch + o, N_CH)), device_id_type=MESH)
 

time: 46.1 us -> 43.9 us (0.952)
  Pallas kernels: 44.1 us -> 42.1 us
    pallas_call x1, Pallas kernels: 44.1 us -> 42.1 us  [on_device(): pl.pallas_call(kernel, out_shape=jax.ShapeDtypeStruct((N_CTX, CHUNK), BF1...]
where the time goes in v6:
time: 43.9 us; the launch traced here: 43.8 us
  Pallas kernels  42.1 us (96%)
  local copies, waits for them, and re-layouts  1.67 us (4%)
    pallas_call x1, Pallas kernels, on_device(): pl.pallas_call(kernel, out_shape=jax.ShapeDtypeStruct((N_CTX, CHUNK), BF1...  42.1 us
    unnamed x1, local copies, waits for them, and re-layouts  1.67 us

profile of v6, /device:TPU:1, one launch (start us, length us, event | category | flops | bytes accessed | tf_op | source)
XLA Modules:
  0.0 43.8 jit_solution(2275274120228104991)
XLA Ops:
  0.0 42.1 %hyena.1 = bf16[64,2048]{1,0:T(8,128)(2,1)} custom-call(bf16[64,2048]{1,0:T(8,128)(2,1)} %v_hbm.1, bf16[64,2048]{1,0:T(8,128)(2,1)} %k_hbm.1, bf16[64,2048]{1,0:T(8,128)(2,1)} %q_hbm.1, f32[64,2048]{1,0:T(8,128)} %f_hbm.1, f32[1,64]{1,0:T(1,128)} %bitcast.3, bf16[64,256]{1,0:T(8,128)(2,1)} %bitcast.2, f32[2,16,256]{2,1,0:T(8,128)} %constant.20.clone.fa_hbm, ...), custom_call_target="tpu_custom_call" | custom-call | tf_op jit(solution)/shard_map/hyena/pallas_call | solution.py:399
  42.1 1.7 %copy.18 = bf16[64,2048]{1,0:T(8,128)(2,1)} copy(bf16[64,2048]{1,0:T(8,128)(2,1)} %hyena.1) | data formatting | bytes 524288

commit v7 on v6

--- a/solution.py
+++ b/solution.py
@@ -323,26 +323,26 @@
             device_id=(peer, to), device_id_type=MESH,
         )
 
-    for first in (0, 2):
-        at = slice(first * 128, first * 128 + 256)
-        y = dot(ph[...], y_hi[:, at]) + dot(plo[...], y_hi[:, at]) + dot(ph[...], y_lo[:, at])
-        for r in range(2):
-            send_y[first + r] = y[:, r * 128 : r * 128 + 128].reshape(N_CTX, PIECES, 128).astype(BF16)
-
-    for to_z in (0, 1, 2, 3, 4, 7, 5, 6):
-
-        def step(i, carry, base=to_z * 8):
-            peer = base + wrap(lane + i, 8)
-            for k in (2, 1, 3):
-                piece_copy(peer, sides[k]).start()
-
-            @pl.when(peer != me)
-            def _():
-                piece_copy(peer, ch).start()
-
-            return carry
-
-        lax.fori_loop(0, 8, step, 0, unroll=2)
+    for part in range(2):
+        rows = slice(part * (A // 2), (part + 1) * (A // 2))
+        half = slice(part * (N_CTX // 2), (part + 1) * (N_CTX // 2))
+        y = dot(ph[rows, :], y_hi[...]) + dot(plo[rows, :], y_hi[...]) + dot(ph[rows, :], y_lo[...])
+        for r in range(N_CH):
+            send_y[r, half] = y[:, r * 128 : r * 128 + 128].reshape(N_CTX // 2, PIECES, 128).astype(BF16)
+        for to_z in ((0, 1, 2, 3), (4, 7, 5, 6))[part]:
+
+            def step(i, carry, base=to_z * 8, part=part, first=int(to_z == 0)):
+                peer = base + (wrap(lane + i, 8) if part else wrap(i + first, 8))
+                for k in (2, 1, 3):
+                    piece_copy(peer, sides[k]).start()
+
+                @pl.when(peer != me)
+                def _():
+                    piece_copy(peer, ch).start()
+
+                return carry
+
+            lax.fori_loop(0, 8, step, 0, unroll=2)
     pltpu.make_async_copy(send_y.at[ch, me], recv_y.at[ch, me], y_recv.at[ch]).start()
 
     three = pl.ds(0, N_CH - 1)

time: 43.9 us -> 42.6 us (0.970)
  the two profiles are of different devices: /device:TPU:1 before, /device:TPU:65 now
where the time goes in v7:
time: 42.6 us; the launch traced here: 42.5 us
  Pallas kernels  40.8 us (96%)
  local copies, waits for them, and re-layouts  1.67 us (4%)
    pallas_call x1, Pallas kernels, on_device(): pl.pallas_call(kernel, out_shape=jax.ShapeDtypeStruct((N_CTX, CHUNK), BF1...  40.8 us
    unnamed x1, local copies, waits for them, and re-layouts  1.67 us

profile of v7, /device:TPU:65, one launch (start us, length us, event | category | flops | bytes accessed | tf_op | source)
XLA Modules:
  0.0 42.5 jit_solution(14548632336455832815)
XLA Ops:
  0.0 40.8 %hyena.1 = bf16[64,2048]{1,0:T(8,128)(2,1)} custom-call(bf16[64,2048]{1,0:T(8,128)(2,1)} %v_hbm.1, bf16[64,2048]{1,0:T(8,128)(2,1)} %k_hbm.1, bf16[64,2048]{1,0:T(8,128)(2,1)} %q_hbm.1, f32[64,2048]{1,0:T(8,128)} %f_hbm.1, f32[1,64]{1,0:T(1,128)} %bitcast.3, bf16[64,256]{1,0:T(8,128)(2,1)} %bitcast.2, f32[2,16,256]{2,1,0:T(8,128)} %constant.20.clone.fa_hbm, ...), custom_call_target="tpu_custom_call" | custom-call | tf_op jit(solution)/shard_map/hyena/pallas_call | solution.py:399
  40.8 1.7 %copy.18 = bf16[64,2048]{1,0:T(8,128)(2,1)} copy(bf16[64,2048]{1,0:T(8,128)(2,1)} %hyena.1) | data formatting | bytes 524288

commit v8 on v7

--- a/solution.py
+++ b/solution.py
@@ -398,7 +398,7 @@
     dma = pltpu.SemaphoreType.DMA
     return pl.pallas_call(
         kernel,
-        out_shape=jax.ShapeDtypeStruct((N_CTX, CHUNK), BF16),
+        out_shape=pltpu.VMEM((N_CTX, CHUNK), BF16),
         in_specs=[pl.BlockSpec(memory_space=pltpu.HBM)] * len(args),
         out_specs=pl.BlockSpec(memory_space=pltpu.VMEM),
         scratch_shapes=copies
@@ -426,7 +426,7 @@
             dma, dma, pltpu.SemaphoreType.REGULAR,
         ],
         compiler_params=pltpu.CompilerParams(
-            collective_id=0, has_side_effects=True, vmem_limit_bytes=56 * 1024 * 1024
+            collective_id=0, has_side_effects=True, vmem_limit_bytes=54 * 1024 * 1024
         ),
         name="hyena",
     )(*args)

time: 42.6 us -> 41 us (0.962)
  local copies, waits for them, and re-layouts: 1.67 us -> 0.71 us
  Pallas kernels: 40.8 us -> 40.2 us
    unnamed x1, local copies, waits for them, and re-layouts: 1.67 us -> 0.71 us
    pallas_call x1, Pallas kernels: 40.8 us -> 40.2 us  [on_device(): pl.pallas_call(kernel, out_shape=pltpu.VMEM((N_CTX, CHUNK), BF16), in_spe...]
where the time goes in v8:
time: 41 us; the launch traced here: 40.9 us
  Pallas kernels  40.2 us (98%)
  local copies, waits for them, and re-layouts  0.71 us (2%)
    pallas_call x1, Pallas kernels, on_device(): pl.pallas_call(kernel, out_shape=pltpu.VMEM((N_CTX, CHUNK), BF16), in_spe...  40.2 us

profile of v8, /device:TPU:65, one launch (start us, length us, event | category | flops | bytes accessed | tf_op | source)
XLA Modules:
  0.0 40.9 jit_solution(6980940447034751303)
XLA Ops:
  0.0 40.2 %hyena.1 = bf16[64,2048]{1,0:T(8,128)(2,1)S(1)} custom-call(bf16[64,2048]{1,0:T(8,128)(2,1)} %v_hbm.1, bf16[64,2048]{1,0:T(8,128)(2,1)} %k_hbm.1, bf16[64,2048]{1,0:T(8,128)(2,1)} %q_hbm.1, f32[64,2048]{1,0:T(8,128)} %f_hbm.1, f32[1,64]{1,0:T(1,128)} %bitcast.3, bf16[64,256]{1,0:T(8,128)(2,1)} %bitcast.2, f32[2,16,256]{2,1,0:T(8,128)} %constant.20.clone.fa_hbm, ...), custom_call_target="tpu_custom_call" | custom-call | tf_op jit(solution)/shard_map/hyena/pallas_call | solution.py:399
  40.2 0.7 %copy.18 = bf16[64,2048]{1,0:T(8,128)(2,1)} copy(bf16[64,2048]{1,0:T(8,128)(2,1)S(1)} %hyena.1) | data formatting | bytes 524288

commit v9 on v8

--- a/solution.py
+++ b/solution.py
@@ -342,7 +342,7 @@
 
                 return carry
 
-            lax.fori_loop(0, 8, step, 0, unroll=2)
+            lax.fori_loop(0, 8, step, 0, unroll=4)
     pltpu.make_async_copy(send_y.at[ch, me], recv_y.at[ch, me], y_recv.at[ch]).start()
 
     three = pl.ds(0, N_CH - 1)

time: 41 us -> 41 us (level)
  no operation moved by 1% of the time
where the time goes in v9:
time: 41 us; the launch traced here: 40.9 us
  Pallas kernels  40.2 us (98%)
  local copies, waits for them, and re-layouts  0.71 us (2%)
    pallas_call x1, Pallas kernels, on_device(): pl.pallas_call(kernel, out_shape=pltpu.VMEM((N_CTX, CHUNK), BF16), in_spe...  40.2 us

profile of v9, /device:TPU:65, one launch (start us, length us, event | category | flops | bytes accessed | tf_op | source)
XLA Modules:
  0.0 40.9 jit_solution(4805057991069619781)
XLA Ops:
  0.0 40.2 %hyena.1 = bf16[64,2048]{1,0:T(8,128)(2,1)S(1)} custom-call(bf16[64,2048]{1,0:T(8,128)(2,1)} %v_hbm.1, bf16[64,2048]{1,0:T(8,128)(2,1)} %k_hbm.1, bf16[64,2048]{1,0:T(8,128)(2,1)} %q_hbm.1, f32[64,2048]{1,0:T(8,128)} %f_hbm.1, f32[1,64]{1,0:T(1,128)} %bitcast.3, bf16[64,256]{1,0:T(8,128)(2,1)} %bitcast.2, f32[2,16,256]{2,1,0:T(8,128)} %constant.20.clone.fa_hbm, ...), custom_call_target="tpu_custom_call" | custom-call | tf_op jit(solution)/shard_map/hyena/pallas_call | solution.py:399
  40.2 0.7 %copy.18 = bf16[64,2048]{1,0:T(8,128)(2,1)} copy(bf16[64,2048]{1,0:T(8,128)(2,1)S(1)} %hyena.1) | data formatting | bytes 524288
